TPU v7x, 32 devices: a whole 2x2x4 slice. The times are simulated.
32 devices in a mesh: ctx: 8 (over z, core), tp: 4 (over y, x).
Axes of the slice: x: 2, y: 2, z: 4, core: 2. Of those that a mesh axis runs over, the one named last changes fastest.
Arguments:
- queries: bfloat16 [2048, 4096], P('ctx', 'tp'), may hold values from -6 to 6
- key_rows: bfloat16 [2048, 4096], P('ctx', 'tp'), may hold values from -6 to 6
- value_rows: bfloat16 [2048, 4096], P('ctx', 'tp'), may hold values from -6 to 6
- segment_ids: int32 [2048], replicated, may hold values from 0 to 3, never falling along the last dimension, each value on 1 to 1024 neighbouring positions
- codebook_ids: int32 [2048, 8], P(('ctx', 'tp')), may hold values from 0 to 2047
- code_table: bfloat16 [8, 2048, 1024], P(None, 'tp'), may hold values from -4 to 4
- input_proj: bfloat16 [4096, 1024], replicated, may hold values from -0.75 to 0.75
- norm_gain: float32 [1024], replicated, may hold values from 0.1 to 1.9
- upstream: bfloat16 [2048, 8, 1024], P(('ctx', 'tp')), may hold values from -3 to 3
Outputs:
- depth_out: bfloat16 [2048, 8, 1024], P(('ctx', 'tp'))
- grad_query: float32 [2048, 4096], P('ctx', 'tp')
- grad_key: float32 [2048, 4096], P('ctx', 'tp')
- grad_value: float32 [2048, 4096], P('ctx', 'tp')
- grad_proj: float32 [4096, 1024], P('tp', 'ctx')
- grad_gain: float32 [1024], P(('ctx', 'tp'))
All inputs are finite; a program needn't handle non-finite values.
Results may differ from a plain program's by a relative error of at most 0.024.
Values may be sent and summed in bfloat16 or wider, within the bound.
No kernel may reach another device: no remote copies, remote signals or barrier semaphores. Data moves between devices by JAX's collectives and lax.ppermute only.
A program may use at most 128 MiB of HBM per device.

v0:
```python
import jax
import jax.numpy as jnp
from jax import lax
from jax.sharding import PartitionSpec as P

HEAD_DIM = 128


NEGATIVE = -1e30
EPSILON = 1e-06


def body(
    queries,
    key_rows,
    value_rows,
    segment_ids,
    codebook_ids,
    code_table,
    input_proj,
    norm_gain,
    upstream,
):
    local_rows = queries.shape[0]
    local_width = queries.shape[1]
    head_count = local_width // HEAD_DIM
    score_scale = HEAD_DIM ** (-0.5)
    ctx_index = lax.axis_index("ctx")
    tp_index = lax.axis_index("tp")
    all_keys, all_values = (
        lax.all_gather(key_rows, "ctx", axis=0, tiled=True),
        lax.all_gather(value_rows, "ctx", axis=0, tiled=True),
    )
    key_total = all_keys.shape[0]
    block_rows = 512
    block_count = key_total // block_rows
    block_list = jnp.arange(block_count, dtype=jnp.int32)
    first_row = ctx_index * local_rows

    def block_scores(query_heads, query_pos, query_seg, block_index):
        key_start = block_index * block_rows
        key_block = lax.dynamic_slice_in_dim(all_keys, key_start, block_rows, 0).reshape(
            block_rows, head_count, HEAD_DIM
        )
        value_block = lax.dynamic_slice_in_dim(all_values, key_start, block_rows, 0).reshape(
            block_rows, head_count, HEAD_DIM
        )
        scores = (
            jnp.einsum("qhd,khd->hqk", query_heads, key_block, preferred_element_type=jnp.float32)
            * score_scale
        )
        key_pos = key_start + jnp.arange(block_rows)
        key_seg = lax.dynamic_slice_in_dim(segment_ids, key_start, block_rows)
        allowed = (key_pos[None, :] <= query_pos[:, None]) & (
            key_seg[None, :] == query_seg[:, None]
        )
        return (jnp.where(allowed[None], scores, NEGATIVE), allowed, key_block, value_block)

    def visit(block_index, last_visible, carried, compute, skipped):
        return lax.cond(block_index * block_rows <= last_visible, compute, skipped, carried)

    def keep_state(state):
        return state

    def describe(query_rows, start_row):
        row_count = query_rows.shape[0]
        query_heads = query_rows.reshape(row_count, head_count, HEAD_DIM)
        query_pos = start_row + jnp.arange(row_count)
        query_seg = lax.dynamic_slice_in_dim(segment_ids, start_row, row_count)
        return (query_heads, query_pos, query_seg, start_row + row_count - 1)

    row_count = queries.shape[0]
    query_heads, query_pos, query_seg, last_visible = describe(queries, first_row)

    def stats_step(carried, block_index):

        def compute(state):
            top_score, row_mass = state
            scores, allowed, key_block, value_block = block_scores(
                query_heads, query_pos, query_seg, block_index
            )
            new_top = jnp.maximum(top_score, jnp.max(scores, axis=2))
            shifted = jnp.where(allowed[None], jnp.exp(scores - new_top[:, :, None]), 0.0)
            return (
                (new_top, row_mass * jnp.exp(top_score - new_top) + jnp.sum(shifted, axis=2)),
                scores,
            )

        def skipped(state):
            return (state, jnp.full((head_count, row_count, block_rows), NEGATIVE, jnp.float32))

        return visit(block_index, last_visible, carried, compute, skipped)

    start_top = jnp.full((head_count, row_count), NEGATIVE, jnp.float32)
    start_mass = jnp.zeros((head_count, row_count), jnp.float32)
    (top_score, row_mass), score_stack = lax.scan(stats_step, (start_top, start_mass), block_list)
    log_norm = top_score + jnp.log(row_mass)

    def output_step(carried, inputs):
        block_index, scores = inputs

        def compute(state):
            key_start = block_index * block_rows
            value_block = lax.dynamic_slice_in_dim(all_values, key_start, block_rows, 0).reshape(
                block_rows, head_count, HEAD_DIM
            )
            weights = jnp.exp(scores - log_norm[:, :, None]).astype(jnp.bfloat16)
            return state + jnp.einsum(
                "hqk,khd->qhd", weights, value_block, preferred_element_type=jnp.float32
            )

        return (visit(block_index, last_visible, carried, compute, keep_state), None)

    start_out = jnp.zeros((row_count, head_count, HEAD_DIM), jnp.float32)
    out_sum, unused = lax.scan(output_step, start_out, (block_list, score_stack))
    group_out = out_sum.reshape(row_count, local_width).astype(jnp.bfloat16)
    attn_out, log_norm = (group_out, log_norm)
    group_codes = lax.all_gather(codebook_ids, "tp", axis=0, tiled=True)
    shard_rows = code_table.shape[1]
    local_codes = group_codes - tp_index * shard_rows
    table_rows = jnp.arange(shard_rows, dtype=jnp.int32)
    selector = (local_codes[:, :, None] == table_rows[None, None, :]).astype(jnp.bfloat16)
    looked = jnp.einsum("tcr,crw->tcw", selector, code_table, preferred_element_type=jnp.float32)
    embedded = lax.psum_scatter(
        looked.astype(jnp.bfloat16), "tp", scatter_dimension=0, tiled=True
    ).astype(jnp.float32)
    w_part = lax.dynamic_slice_in_dim(input_proj, tp_index * local_width, local_width, 0)
    projected = lax.psum_scatter(
        jnp.dot(attn_out, w_part, preferred_element_type=jnp.float32).astype(jnp.bfloat16),
        "tp",
        scatter_dimension=0,
        tiled=True,
    ).astype(jnp.float32)
    hidden = projected[:, None, :] + embedded
    inverse = lax.rsqrt(jnp.mean(hidden * hidden, axis=2, keepdims=True) + EPSILON)
    normed = hidden * inverse
    depth_out = (normed * norm_gain).astype(jnp.bfloat16)
    cotangent = upstream.astype(jnp.float32)
    gain_term = jnp.sum(cotangent * normed, axis=(0, 1))
    grad_gain = lax.psum_scatter(gain_term, ("ctx", "tp"), scatter_dimension=0, tiled=True)
    grad_normed = cotangent * norm_gain
    grad_hidden = inverse * (
        grad_normed - normed * jnp.mean(grad_normed * normed, axis=2, keepdims=True)
    )
    grad_sum = jnp.sum(grad_hidden, axis=1).astype(jnp.bfloat16)
    gathered = lax.all_gather(grad_sum, "tp", axis=0, tiled=True)
    grad_attn = lax.dot_general(
        gathered, w_part, (((1,), (1,)), ((), ())), preferred_element_type=jnp.float32
    ).astype(jnp.bfloat16)
    weight_term = lax.dot_general(
        attn_out, gathered, (((0,), (0,)), ((), ())), preferred_element_type=jnp.float32
    )
    grad_proj = lax.psum_scatter(
        weight_term.astype(jnp.bfloat16), "ctx", scatter_dimension=1, tiled=True
    ).astype(jnp.float32)
    backward_row_count = queries.shape[0]
    backward_query_heads, backward_query_pos, backward_query_seg, backward_last_visible = describe(
        queries, first_row
    )
    grad_heads = grad_attn.reshape(backward_row_count, head_count, HEAD_DIM)
    out_heads = attn_out.reshape(backward_row_count, head_count, HEAD_DIM)
    row_delta = jnp.sum(grad_heads.astype(jnp.float32) * out_heads.astype(jnp.float32), axis=2).T

    def back_step(carried, block_index):

        def compute(query_total):
            scores, allowed, key_block, value_block = block_scores(
                backward_query_heads, backward_query_pos, backward_query_seg, block_index
            )
            probs = jnp.exp(scores - log_norm[:, :, None])
            weights = probs.astype(jnp.bfloat16)
            grad_prob = jnp.einsum(
                "qhd,khd->hqk", grad_heads, value_block, preferred_element_type=jnp.float32
            )
            grad_score = (probs * (grad_prob - row_delta[:, :, None])).astype(jnp.bfloat16)
            query_total = query_total + jnp.einsum(
                "hqk,khd->qhd", grad_score, key_block, preferred_element_type=jnp.float32
            )
            key_grad = (
                jnp.einsum(
                    "hqk,qhd->khd",
                    grad_score,
                    backward_query_heads,
                    preferred_element_type=jnp.float32,
                )
                * score_scale
            )
            value_grad = jnp.einsum(
                "hqk,qhd->khd", weights, grad_heads, preferred_element_type=jnp.float32
            )
            return (
                query_total,
                (
                    key_grad.reshape(block_rows, local_width),
                    value_grad.reshape(block_rows, local_width),
                ),
            )

        def skipped(query_total):
            empty_block = jnp.zeros((block_rows, local_width), jnp.float32)
            return (query_total, (empty_block, empty_block))

        return visit(block_index, backward_last_visible, carried, compute, skipped)

    start_grad = jnp.zeros((backward_row_count, head_count, HEAD_DIM), jnp.float32)
    query_sum, (key_stack, value_stack) = lax.scan(back_step, start_grad, block_list)
    group_query = (query_sum * score_scale).reshape(backward_row_count, local_width)
    key_acc = key_stack.reshape(key_total, local_width)
    value_acc = value_stack.reshape(key_total, local_width)
    grad_key, grad_value = (
        lax.psum_scatter(
            key_acc.astype(jnp.bfloat16), "ctx", scatter_dimension=0, tiled=True
        ).astype(jnp.float32),
        lax.psum_scatter(
            value_acc.astype(jnp.bfloat16), "ctx", scatter_dimension=0, tiled=True
        ).astype(jnp.float32),
    )
    return (depth_out, group_query, grad_key, grad_value, grad_proj, grad_gain)


def solution(mesh):
    return jax.shard_map(
        body,
        mesh=mesh,
        in_specs=(
            P("ctx", "tp"),
            P("ctx", "tp"),
            P("ctx", "tp"),
            P(),
            P(("ctx", "tp"), None),
            P(None, "tp", None),
            P(),
            P(),
            P(("ctx", "tp"), None, None),
        ),
        out_specs=(
            P(("ctx", "tp"), None, None),
            P("ctx", "tp"),
            P("ctx", "tp"),
            P("ctx", "tp"),
            P("tp", "ctx"),
            P(("ctx", "tp")),
        ),
        check_vma=False,
    )
```

profile of v0, /device:TPU:9, one launch (start us, length us, event | category | flops | bytes accessed | tf_op | source)
XLA Modules:
  0.0 420.7 jit_solution(3233055614113702166)
XLA Ops:
  13.1 45.2 %all-gather.6.cloned.1.call-done = bf16[2048,1024]{0,1:T(8,128)(2,1)} async-done(((bf16[256,1024]{0,1:T(8,128)(2,1)}), bf16[2048,1024]{0,1:T(8,128)(2,1)}) %all-gather.6.cloned.1.call-update) | async-done | bytes 4194320 | tf_op jit(solution)/shard_map/all_gather | solution.py:31
  58.3 62.0 %while.47 = (s32[]{:T(128)}, f32[8,256]{1,0:T(8,128)S(1)}, f32[8,256]{1,0:T(8,128)S(1)}, f32[4,8,256,512]{3,2,1,0:T(8,128)}, s32[4]{0:T(128)S(1)}, /*index=5*/s3...) while((s32[]{:T(128)}, f32[8,256]{1,0:T(8,128)S(1)}, ...), condition=%wide.region_5.6_spmd.clone, body=%wide.region_0.5_spmd.clone.sunk | while | flops 277222144 | bytes 33546064 | solution.py:96
  59.6 6.2 %conditional.9 = (f32[8,256]{1,0:T(8,128)S(1)}, f32[8,256]{1,0:T(8,128)S(1)}, f32[1,8,256,512]{2,3,1,0:T(8,128)}) conditional(s32[]{:T(128)} %convert_element_type.155, (f32[8,256]{1,0:T(8,128)S(1)}, f32[8,256]{1,0:T(8,128)S(1)}) %tuple.111, (s32[]{:T(128)}, s32[]{:T(128)}, s32[2048]{0:T(1024)S(1)}, s32[256]{0:T(256)S(1)}, ...), branch_computations={%region_1.1_spmd, %region_2.4_spmd} | conditional | flops 277222144 | bytes 16767062 | solution.py:60
  62.8 2.9 fusion.4
  65.7 5.5 %copy.97 = f32[1,8,256,512]{3,2,1,0:T(8,128)} copy(f32[1,8,256,512]{2,3,1,0:T(8,128)} %get-tuple-element.759) | data formatting | bytes 8388608 | tf_op jit(solution)/shard_map/while/body/jit(dynamic_update_index_in_dim)/dynamic_update_slice | solution.py:96
  71.3 4.6 %constant_dynamic-update-slice_fusion.5 = f32[4,8,256,512]{3,2,1,0:T(8,128)} fusion(f32[4,8,256,512]{3,2,1,0:T(8,128)} %get-tuple-element.808, f32[1,8,256,512]{3,2,1,0:T(8,128)} %copy.97, s32[]{:T(128)} %get-tuple-element.805), kind=kLoop, calls=%fused_computation.41.clone.1 | loop fusion | bytes 8389120 | tf_op jit(solution)/shard_map/while/body/jit(dynamic_update_index_in_dim)/dynamic_update_slice | solution.py:96
  77.1 6.2 %conditional.9 = (f32[8,256]{1,0:T(8,128)S(1)}, f32[8,256]{1,0:T(8,128)S(1)}, f32[1,8,256,512]{2,3,1,0:T(8,128)}) conditional(s32[]{:T(128)} %convert_element_type.155, (f32[8,256]{1,0:T(8,128)S(1)}, f32[8,256]{1,0:T(8,128)S(1)}) %tuple.111, (s32[]{:T(128)}, s32[]{:T(128)}, s32[2048]{0:T(1024)S(1)}, s32[256]{0:T(256)S(1)}, ...), branch_computations={%region_1.1_spmd, %region_2.4_spmd} | conditional | flops 277222144 | bytes 16767062 | solution.py:60
  83.2 5.4 %copy.97 = f32[1,8,256,512]{3,2,1,0:T(8,128)} copy(f32[1,8,256,512]{2,3,1,0:T(8,128)} %get-tuple-element.759) | data formatting | bytes 8388608 | tf_op jit(solution)/shard_map/while/body/jit(dynamic_update_index_in_dim)/dynamic_update_slice | solution.py:96
  88.6 4.6 %constant_dynamic-update-slice_fusion.5 = f32[4,8,256,512]{3,2,1,0:T(8,128)} fusion(f32[4,8,256,512]{3,2,1,0:T(8,128)} %get-tuple-element.808, f32[1,8,256,512]{3,2,1,0:T(8,128)} %copy.97, s32[]{:T(128)} %get-tuple-element.805), kind=kLoop, calls=%fused_computation.41.clone.1 | loop fusion | bytes 8389120 | tf_op jit(solution)/shard_map/while/body/jit(dynamic_update_index_in_dim)/dynamic_update_slice | solution.py:96
  96.8 5.4 %copy.97 = f32[1,8,256,512]{3,2,1,0:T(8,128)} copy(f32[1,8,256,512]{2,3,1,0:T(8,128)} %get-tuple-element.759) | data formatting | bytes 8388608 | tf_op jit(solution)/shard_map/while/body/jit(dynamic_update_index_in_dim)/dynamic_update_slice | solution.py:96
  102.2 4.6 %constant_dynamic-update-slice_fusion.5 = f32[4,8,256,512]{3,2,1,0:T(8,128)} fusion(f32[4,8,256,512]{3,2,1,0:T(8,128)} %get-tuple-element.808, f32[1,8,256,512]{3,2,1,0:T(8,128)} %copy.97, s32[]{:T(128)} %get-tuple-element.805), kind=kLoop, calls=%fused_computation.41.clone.1 | loop fusion | bytes 8389120 | tf_op jit(solution)/shard_map/while/body/jit(dynamic_update_index_in_dim)/dynamic_update_slice | solution.py:96
  110.4 5.4 %copy.97 = f32[1,8,256,512]{3,2,1,0:T(8,128)} copy(f32[1,8,256,512]{2,3,1,0:T(8,128)} %get-tuple-element.759) | data formatting | bytes 8388608 | tf_op jit(solution)/shard_map/while/body/jit(dynamic_update_index_in_dim)/dynamic_update_slice | solution.py:96
  115.7 4.6 %constant_dynamic-update-slice_fusion.5 = f32[4,8,256,512]{3,2,1,0:T(8,128)} fusion(f32[4,8,256,512]{3,2,1,0:T(8,128)} %get-tuple-element.808, f32[1,8,256,512]{3,2,1,0:T(8,128)} %copy.97, s32[]{:T(128)} %get-tuple-element.805), kind=kLoop, calls=%fused_computation.41.clone.1 | loop fusion | bytes 8389120 | tf_op jit(solution)/shard_map/while/body/jit(dynamic_update_index_in_dim)/dynamic_update_slice | solution.py:96
  120.4 15.7 %while.46 = (s32[]{:T(128)}, f32[256,8,128]{0,2,1:T(8,128)S(1)}, s32[4]{0:T(128)S(1)}, s32[]{:T(128)}, bf16[2048,1024]{0,1:T(8,128)(2,1)}, /*index=5*/f32[4,8,25...) while((s32[]{:T(128)}, f32[256,8,128]{0,2,1:T(8,128)S(1)}, s32[4]{0:T(128)S(1)}, s32[]{:T(128)}, ...), condition=%wide.region_9.10_spmd, body=%wide.region_6.9_spmd.sunk | while | flops 270794752 | bytes 9446125 | solution.py:115
  121.7 5.3 %conditional.8 = (f32[256,8,128]{0,2,1:T(8,128)S(1)}) conditional(s32[]{:T(128)} %convert_element_type.154, f32[256,8,128]{0,2,1:T(8,128)S(1)} %get-tuple-element.841, (s32[]{:T(128)}, bf16[2048,1024]{0,1:T(8,128)(2,1)}, f32[4,8,256,512]{3,2,1,0:T(8,128)}, s32[]{:T(128)}, f32[8,256]{1,0:T(8,128)S(1)}, /*index=5*/f32[256,8,128]{0,2,1:T(8,128)S(1)}) %tuple.109), branch_computations={%region_7.7_spmd, %region_8.8_spmd} | conditional | flops 270794752 | bytes 9445946 | solution.py:60
  123.6 3.4 fusion.14
  128.3 5.3 %conditional.8 = (f32[256,8,128]{0,2,1:T(8,128)S(1)}) conditional(s32[]{:T(128)} %convert_element_type.154, f32[256,8,128]{0,2,1:T(8,128)S(1)} %get-tuple-element.841, (s32[]{:T(128)}, bf16[2048,1024]{0,1:T(8,128)(2,1)}, f32[4,8,256,512]{3,2,1,0:T(8,128)}, s32[]{:T(128)}, f32[8,256]{1,0:T(8,128)S(1)}, /*index=5*/f32[256,8,128]{0,2,1:T(8,128)S(1)}) %tuple.109), branch_computations={%region_7.7_spmd, %region_8.8_spmd} | conditional | flops 270794752 | bytes 9445946 | solution.py:60
  130.2 3.4 fusion.14
  136.2 3.1 fusion.44
  139.5 4.6 %all-gather = s32[4,64,8]{1,2,0:T(8,128)S(1)} all-gather(s32[1,64,8]{1,2,0:T(8,128)S(1)} %bitcast.113), channel_id=1, replica_groups=mesh['ctx'=8,'tp'=4] {'tp'}, dimensions={0}, use_global_device_ids=true | all-gather | bytes 10240 | tf_op jit(solution)/shard_map/all_gather | solution.py:118
  144.2 7.4 %convert_bitcast_fusion = bf16[256,8,1024]{2,0,1:T(8,128)(2,1)} fusion(bf16[8,512,1024]{2,1,0:T(8,128)(2,1)} %param.26, s32[256,8]{0,1:T(8,128)S(1)} %reshape.187), kind=kOutput, calls=%fused_computation.44 | convolution fusion | flops 2150629376 | bytes 12591104 | tf_op jit(solution)/shard_map/tcr,crw->tcw/dot_general | solution.py:123
  151.7 29.9 %reduce-scatter.8.cloned.1.call-done = bf16[64,1024]{1,0:T(8,128)(2,1)} async-done(((bf16[256,1024]{1,0:T(8,128)(2,1)}), bf16[64,1024]{1,0:T(8,128)(2,1)}) %reduce-scatter.8.cloned.1.call-update) | async-done | bytes 131088 | tf_op jit(solution)/shard_map/reduce_scatter | solution.py:128
  182.6 55.0 %reduce-scatter.10.cloned.1.call-done = bf16[64,8,1024]{2,0,1:T(8,128)(2,1)} async-done(((bf16[256,8,1024]{2,0,1:T(8,128)(2,1)}), bf16[64,8,1024]{2,0,1:T(8,128)(2,1)}) %reduce-scatter.10.cloned.1.call-update) | async-done | bytes 1048592 | tf_op jit(solution)/shard_map/reduce_scatter | solution.py:124
  243.9 8.1 %all_gather.15 = bf16[256,1024]{1,0:T(8,128)(2,1)S(1)} all-gather(bf16[64,1024]{1,0:T(8,128)(2,1)S(1)} %get-tuple-element.561), channel_id=1, replica_groups=mesh['ctx'=8,'tp'=4] {'tp'}, dimensions={0}, use_global_device_ids=true | all-gather | bytes 655360 | tf_op jit(solution)/shard_map/all_gather | solution.py:146
  254.0 3.9 copy.83
  261.7 26.6 %while.48 = (s32[]{:T(128)}, f32[256,8,128]{0,2,1:T(8,128)}, bf16[4,512,1024]{1,2,0:T(8,128)(2,1)}, bf16[4,512,1024]{1,2,0:T(8,128)(2,1)}, s32[4]{0:T(128)S(1)},...) while((s32[]{:T(128)}, f32[256,8,128]{0,2,1:T(8,128)}, ...), condition=%wide.region_19.20_spmd.clone, body=%wide.region_16.19_spmd.clone.sunk | while | flops 1354367744 | bytes 45522864 | solution.py:206
  263.0 7.6 %conditional.10 = (f32[256,8,128]{0,2,1:T(8,128)}, bf16[1,512,1024]{1,2,0:T(8,128)(2,1)S(1)}, bf16[1,512,1024]{1,2,0:T(8,128)(2,1)S(1)}) conditional(s32[]{:T(128)} %convert_element_type.156, f32[256,8,128]{0,2,1:T(8,128)} %get-tuple-element.876, (s32[]{:T(128)}, bf16[2048,1024]{0,1:T(8,128)(2,1)}, s32[]{:T(128)}, s32[2048]{0:T(1024)S(1)}, ...), branch_computations={%region_17.17_spmd, %region_18.18_spmd} | conditional | flops 1354367744 | bytes 41326736 | solution.py:60
  273.4 7.6 %conditional.10 = (f32[256,8,128]{0,2,1:T(8,128)}, bf16[1,512,1024]{1,2,0:T(8,128)(2,1)S(1)}, bf16[1,512,1024]{1,2,0:T(8,128)(2,1)S(1)}) conditional(s32[]{:T(128)} %convert_element_type.156, f32[256,8,128]{0,2,1:T(8,128)} %get-tuple-element.876, (s32[]{:T(128)}, bf16[2048,1024]{0,1:T(8,128)(2,1)}, s32[]{:T(128)}, s32[2048]{0:T(1024)S(1)}, ...), branch_computations={%region_17.17_spmd, %region_18.18_spmd} | conditional | flops 1354367744 | bytes 41326736 | solution.py:60
  288.4 6.3 %copy.72 = bf16[4,512,1024]{2,1,0:T(8,128)(2,1)} copy(bf16[4,512,1024]{1,2,0:T(8,128)(2,1)} %get-tuple-element.297) | data formatting | bytes 8388608 | tf_op jit(solution)/shard_map/convert_element_type | solution.py:215
  294.7 6.3 %copy.71 = bf16[4,512,1024]{2,1,0:T(8,128)(2,1)} copy(bf16[4,512,1024]{1,2,0:T(8,128)(2,1)} %get-tuple-element.296) | data formatting | bytes 8388608 | tf_op jit(solution)/shard_map/convert_element_type | solution.py:212
  306.5 57.3 %all-reduce = f32[1024]{0:T(1024)S(1)} all-reduce(f32[1024]{0:T(1024)S(1)} %get-tuple-element.485), channel_id=7, replica_groups=mesh['ctx'=8,'tp'=4] {'ctx','tp'}, use_global_device_ids=true, to_apply=%region_24.25.clone | all-reduce | flops 1024 | bytes 8192
  368.5 43.3 %reduce-scatter.12.cloned.1.call-done = bf16[256,1024]{1,0:T(8,128)(2,1)} async-done(((bf16[2048,1024]{1,0:T(8,128)(2,1)}), bf16[256,1024]{1,0:T(8,128)(2,1)}) %reduce-scatter.12.cloned.1.call-update) | async-done | bytes 524304 | tf_op jit(solution)/shard_map/reduce_scatter | solution.py:211
  (152 shorter events, 78.7 us)
Async XLA Ops:
  7.2 5.8 %copy-start.5 = (s32[2048]{0:T(1024)S(1)}, s32[2048]{0:T(1024)}, u32[]{:S(2)}) copy-start(s32[2048]{0:T(1024)} %param.24) | copy-start | bytes 24580
  7.2 51.1 %all-gather.6.cloned.1.call-start = ((), (), s32[]{:S(2)}) async-start(), calls=%async_computation.6 | async-start | bytes 4718592 | tf_op jit(solution)/shard_map/all_gather | solution.py:31
  9.3 111.0 %all-gather.4.cloned.1.call-start = ((), (), s32[]{:S(2)}) async-start(), calls=%async_computation.5 | async-start | bytes 4718592 | tf_op jit(solution)/shard_map/all_gather | solution.py:32
  11.4 170.2 %reduce-scatter.8.cloned.1.call-start = ((), (), s32[]{:S(2)}) async-start(), calls=%async_computation.7 | async-start | bytes 655360 | tf_op jit(solution)/shard_map/reduce_scatter | solution.py:128
  136.2 3.3 copy-start.7
  139.4 98.2 %reduce-scatter.10.cloned.1.call-start = ((), (), s32[]{:S(2)}) async-start(), calls=%async_computation.8 | async-start | bytes 5242880 | tf_op jit(solution)/shard_map/reduce_scatter | solution.py:124
  151.6 87.6 %copy-start.4 = (bf16[64,8,1024]{2,1,0:T(8,128)(2,1)S(1)}, bf16[64,8,1024]{2,1,0:T(8,128)(2,1)}, u32[]{:S(2)}) copy-start(bf16[64,8,1024]{2,1,0:T(8,128)(2,1)} %param.29) | copy-start | bytes 3145732
  151.6 87.6 %copy-start.6 = (f32[1024]{0:T(1024)S(1)}, f32[1024]{0:T(1024)}, u32[]{:S(2)}) copy-start(f32[1024]{0:T(1024)} %param.28) | copy-start | bytes 12292
  151.7 212.7 %reduce-scatter.16.cloned.1.call-start = ((), (), s32[]{:S(2)}) async-start(), calls=%async_computation.11 | async-start | bytes 2359296
  237.6 4.1 copy-start.3
  257.9 108.5 %reduce-scatter.14.cloned.1.call-start = ((), (), s32[]{:S(2)}) async-start(), calls=%async_computation.10 | async-start | bytes 4718592 | tf_op jit(solution)/shard_map/reduce_scatter | solution.py:214
  266.4 2.3 copy-start
  269.3 1.3 copy-start.1
  276.8 2.3 copy-start
  279.7 1.3 copy-start.1
  294.7 117.0 %reduce-scatter.12.cloned.1.call-start = ((), (), s32[]{:S(2)}) async-start(), calls=%async_computation.9 | async-start | bytes 4718592 | tf_op jit(solution)/shard_map/reduce_scatter | solution.py:211
  301.1 1.2 copy-start.2
Sparse Core Ops, SparseCore 0:
  10.2 48.0 all-gather.5
  60.5 46.0 all-gather.3
  139.5 42.0 reduce-scatter.7
  184.7 52.8 reduce-scatter.9
  258.0 32.4 reduce-scatter.15
  294.8 66.3 reduce-scatter.13
  363.5 48.1 reduce-scatter.11
where the time goes:
time: 426 us; the launch traced here: 421 us
  waiting for transfers between devices  174 us (41%)
  local copies, waits for them, and re-layouts  97.7 us (23%)
  blocking collectives  70.1 us (16%)
  matrix products  33.1 us (8%)
  other arithmetic  19.2 us (5%)
  between operations  14.3 us (3%)
  loops' own time  12.4 us (3%)
    unnamed x1, blocking collectives  57.3 us
    reduce_scatter x1, waiting for transfers between devices, body(): lax.psum_scatter(looked.astype(jnp.bfloat16), 'tp', scatter_dimension=0,...  55 us
    all_gather x1, waiting for transfers between devices, body(): lax.all_gather(key_rows, 'ctx', axis=0, tiled=True)  45.2 us
    reduce_scatter x1, waiting for transfers between devices, body(): lax.psum_scatter(key_acc.astype(jnp.bfloat16), 'ctx', scatter_dimension=0...  43.3 us
    dynamic_update_slice x8, local copies, waits for them, and re-layouts, body(): lax.scan(stats_step, (start_top, start_mass), block_list)  40.1 us
    reduce_scatter x1, waiting for transfers between devices, body(): lax.psum_scatter(jnp.dot(attn_out, w_part, preferred_element_type=jnp.flo...  29.9 us
    unnamed x21, local copies, waits for them, and re-layouts  15.4 us
  transfers between devices with their start and end apart: 7, of which 4 were waited for; matrix products, arithmetic and copies ran while one was open for 28% of the time, Pallas kernels for 0%

commit v1 on v0

--- a/solution.py
+++ b/solution.py
@@ -1,6 +1,10 @@
+import functools
+
 import jax
 import jax.numpy as jnp
 from jax import lax
+from jax.experimental import pallas as pl
+from jax.experimental.pallas import tpu as pltpu
 from jax.sharding import PartitionSpec as P
 
 HEAD_DIM = 128
@@ -8,9 +12,337 @@
 
 NEGATIVE = -1e30
 EPSILON = 1e-06
-
-
-def body(
+LOG2_E = 1.4426950408889634
+SEGMENT_VALUES = 4
+VMEM_BYTES = 50 << 20
+F32 = jnp.float32
+BF16 = jnp.bfloat16
+
+
+def dot(a, b, a_dim, b_dim):
+    return lax.dot_general(a, b, (((a_dim,), (b_dim,)), ((), ())), preferred_element_type=F32)
+
+
+def call(kernel, name, ids, inputs, out_shapes, scratch=(), in_specs=None, out_specs=None, grid=(1,)):
+    def whole(shape):
+        return pl.BlockSpec(shape, lambda step, ids: (0,) * len(shape))
+
+    if in_specs is None:
+        in_specs = {}
+    if out_specs is None:
+        out_specs = {}
+    return pl.pallas_call(
+        kernel,
+        name=name,
+        out_shape=[jax.ShapeDtypeStruct(shape, dtype) for shape, dtype in out_shapes],
+        grid_spec=pltpu.PrefetchScalarGridSpec(
+            num_scalar_prefetch=1,
+            grid=grid,
+            in_specs=[in_specs.get(n, whole(x.shape)) for n, x in enumerate(inputs)],
+            out_specs=[out_specs.get(n, whole(shape)) for n, (shape, _) in enumerate(out_shapes)],
+            scratch_shapes=list(scratch),
+        ),
+        compiler_params=pltpu.CompilerParams(vmem_limit_bytes=VMEM_BYTES),
+    )(ids, *inputs)
+
+
+def offset(index, width):
+    return pl.multiple_of(index * width, width)
+
+
+def pack_kernel(n, width, ids, q_ref, k_ref, v_ref, *outs):
+    me = ids[0]
+    for i in range(n):
+        columns = pl.ds(offset(me ^ i, width), width)
+        for part, ref in enumerate((q_ref, k_ref, v_ref)):
+            outs[i][part] = ref[:, columns]
+
+
+def segment_starts(seg):
+    first = jnp.zeros_like(seg)
+    for value in range(SEGMENT_VALUES - 1):
+        count = jnp.sum((seg == value).astype(jnp.int32), axis=1, keepdims=True)
+        first = first + jnp.where(seg > value, count, 0)
+    return first
+
+
+def visible(starts, low, count, first, rows):
+    key_pos = low + lax.broadcasted_iota(jnp.int32, (count, rows), 0)
+    query_pos = first + lax.broadcasted_iota(jnp.int32, (count, rows), 1)
+    return (key_pos >= starts[:, first : first + rows]) & (key_pos <= query_pos)
+
+
+def forward_kernel(n, rows, window, factor, ids, seg_ref, *refs):
+    pieces, outs = refs[:n], refs[n : 2 * n]
+    out_ref, norm_ref, q_s, k_s, v_s = refs[2 * n :]
+    me = ids[0]
+    for i in range(n):
+        place = pl.ds(offset(me ^ i, rows), rows)
+        q_s[place, :] = pieces[i][0]
+        k_s[place, :] = pieces[i][1]
+        v_s[place, :] = pieces[i][2]
+    starts = segment_starts(seg_ref[...])
+    for block in range(n):
+        first, low = block * rows, max(0, block - window) * rows
+        count = first + rows - low
+        scores = dot(k_s[low : low + count, :], q_s[first : first + rows, :], 1, 1) * factor
+        scores = jnp.where(visible(starts, low, count, first, rows), scores, NEGATIVE)
+        top = jnp.max(scores, axis=0, keepdims=True)
+        mass = jnp.exp2(scores - top)
+        total = jnp.sum(mass, axis=0, keepdims=True)
+        mixed = dot(v_s[low : low + count, :], mass.astype(BF16), 0, 0) / total
+        out_ref[first : first + rows, :] = mixed.T.astype(BF16)
+        norm_ref[:, first : first + rows] = top + jnp.log2(total)
+    for i in range(n):
+        outs[i][...] = out_ref[pl.ds(offset(me ^ i, rows), rows), :]
+
+
+def backward_kernel(n, rows, window, factor, scale, ids, seg_ref, norm_ref, out_ref, *refs):
+    pieces, grads, outs = refs[:n], refs[n : 2 * n], refs[2 * n : 3 * n]
+    q_s, k_s, v_s, g_s, dq_s, dk_s, dv_s = refs[3 * n :]
+    me = ids[0]
+    for i in range(n):
+        place = pl.ds(offset(me ^ i, rows), rows)
+        q_s[place, :] = pieces[i][0]
+        k_s[place, :] = pieces[i][1]
+        v_s[place, :] = pieces[i][2]
+        g_s[place, :] = grads[i][...]
+    starts = segment_starts(seg_ref[...])
+    for block in range(n):
+        first, low = block * rows, max(0, block - window) * rows
+        count = first + rows - low
+        keys, query, grad = k_s[low : low + count, :], q_s[first : first + rows, :], g_s[first : first + rows, :]
+        scores = dot(keys, query, 1, 1) * factor - norm_ref[:, first : first + rows]
+        probs = jnp.exp2(jnp.where(visible(starts, low, count, first, rows), scores, NEGATIVE))
+        product = grad.astype(F32) * out_ref[first : first + rows, :].astype(F32)
+        delta = jnp.sum(product.T, axis=0, keepdims=True)
+        score_grad = (probs * (dot(v_s[low : low + count, :], grad, 1, 1) - delta)).astype(BF16)
+        dq_s[first : first + rows, :] = (dot(keys, score_grad, 0, 0).T * scale).astype(BF16)
+        key_grad = dot(score_grad, query, 1, 0)
+        value_grad = dot(probs.astype(BF16), grad, 1, 0)
+        if count > rows:
+            dk_s[low:first, :] += key_grad[: count - rows]
+            dv_s[low:first, :] += value_grad[: count - rows]
+        dk_s[first : first + rows, :] = key_grad[count - rows :]
+        dv_s[first : first + rows, :] = value_grad[count - rows :]
+    for i in range(n):
+        place = pl.ds(offset(me ^ i, rows), rows)
+        outs[i][0] = dq_s[place, :]
+        outs[i][1] = (dk_s[place, :] * scale).astype(BF16)
+        outs[i][2] = dv_s[place, :].astype(BF16)
+
+
+def project_kernel(n, t, ids, w_ref, *refs):
+    pieces, attn_ref, outs, total = refs[:n], refs[n], refs[n + 1 : n + 1 + t], refs[n + 1 + t]
+    me, shard = ids[0], ids[1]
+    width = pieces[0].shape[1]
+    for i in range(n):
+        attn_ref[:, pl.ds(offset(me ^ i, width), width)] = pieces[i][...]
+    total[...] = dot(attn_ref[...], w_ref[...], 1, 0).astype(BF16)
+    rows = outs[0].shape[0]
+    for i in range(t):
+        outs[i][...] = total[pl.ds(offset(shard ^ i, rows), rows), :]
+
+
+def lookup_kernel(t, ids, table_ref, *refs):
+    codes, outs = refs[:t], refs[t:]
+    book = pl.program_id(0)
+    shard_rows, rows = table_ref.shape[1], codes[0].shape[0]
+    picks = []
+    for i in range(t):
+        lanes = lax.broadcasted_iota(jnp.int32, codes[i].shape, 1)
+        code = jnp.sum(jnp.where(lanes == book, codes[i][...], 0), axis=1, keepdims=True)
+        entry = lax.broadcasted_iota(jnp.int32, (rows, shard_rows), 1) + ids[1] * shard_rows
+        picks.append((entry == code).astype(F32).astype(BF16))
+    found = dot(jnp.concatenate(picks, axis=0), table_ref[0], 1, 0).astype(BF16)
+    for i in range(t):
+        outs[i][0] = found[i * rows : (i + 1) * rows]
+
+
+def depth_kernel(t, books, ids, gain_ref, embed_ref, up_ref, *refs):
+    parts = refs[:t]
+    depth_ref, sum_ref, gain_out_ref = refs[t:]
+    projected = parts[0][...].astype(F32)
+    for i in range(1, t):
+        projected = projected + parts[i][...].astype(F32)
+    gain = gain_ref[...]
+    grad_sum = jnp.zeros_like(projected)
+    gain_sum = jnp.zeros_like(projected)
+    for book in range(books):
+        hidden = projected + embed_ref[book].astype(F32)
+        inverse = lax.rsqrt(jnp.mean(hidden * hidden, axis=1, keepdims=True) + EPSILON)
+        normed = hidden * inverse
+        depth_ref[book] = (normed * gain).astype(BF16)
+        cotangent = up_ref[book].astype(F32)
+        gain_sum = gain_sum + cotangent * normed
+        grad = cotangent * gain
+        grad_sum = grad_sum + inverse * (grad - normed * jnp.mean(grad * normed, axis=1, keepdims=True))
+    sum_ref[...] = grad_sum.astype(BF16)
+    gain_out_ref[...] = jnp.sum(gain_sum, axis=0, keepdims=True)
+
+
+def grad_attn_kernel(n, t, ids, w_ref, *refs):
+    parts, sum_ref, outs, total = refs[:t], refs[t], refs[t + 1 : t + 1 + n], refs[t + 1 + n]
+    me, shard = ids[0], ids[1]
+    rows, width = parts[0].shape[0], outs[0].shape[1]
+    for i in range(t):
+        sum_ref[pl.ds(offset(shard ^ i, rows), rows), :] = parts[i][...]
+    total[...] = dot(sum_ref[...], w_ref[...], 1, 1).astype(BF16)
+    for i in range(n):
+        outs[i][...] = total[:, pl.ds(offset(me ^ i, width), width)]
+
+
+def grad_proj_kernel(n, ids, attn_ref, sum_ref, send_ref, *refs):
+    keeps, total = refs[: n // 2], refs[n // 2]
+    me = ids[0]
+    width = keeps[0].shape[1]
+    total[...] = dot(attn_ref[...], sum_ref[...], 0, 0).astype(BF16)
+    for i in range(n // 2):
+        mine = me ^ (2 * i)
+        keeps[i][...] = total[:, pl.ds(offset(mine, width), width)]
+        send_ref[i] = total[:, pl.ds(offset(mine ^ 1, width), width)]
+
+
+def assemble_kernel(n, ids, *refs):
+    pieces, outs = refs[:n], refs[n:]
+    me = ids[0]
+    width = pieces[0].shape[2]
+    for i in range(n):
+        columns = pl.ds(offset(me ^ i, width), width)
+        for part in range(3):
+            outs[part][:, columns] = pieces[i][part].astype(F32)
+
+
+def swap(x, axis, count, i):
+    return lax.ppermute(x, axis, [(b, b ^ i) for b in range(count)])
+
+
+def swap_all(parts, axis, count):
+    return [parts[0]] + [swap(parts[i], axis, count, i) for i in range(1, count)]
+
+
+def scatter_sum(x, axis, count):
+    index = lax.axis_index(axis)
+    step = count // 2
+    while step:
+        half = x.shape[0] // 2
+        bit = (index // step) % 2
+        kept = lax.dynamic_slice_in_dim(x, bit * half, half, 0)
+        sent = lax.dynamic_slice_in_dim(x, (1 - bit) * half, half, 0)
+        x = kept + swap(sent, axis, count, step)
+        step //= 2
+    return x
+
+
+def heads_body(n, t, queries, key_rows, value_rows, segment_ids, codebook_ids, code_table, input_proj, norm_gain, upstream):
+    rows, width = queries.shape
+    frames = segment_ids.shape[0]
+    books, shard_rows, depth = code_table.shape
+    local = codebook_ids.shape[0]
+    window = -(-(frames // 2 - 1) // rows)
+    scale = HEAD_DIM ** (-0.5)
+    factor = scale * LOG2_E
+    ids = jnp.stack([lax.axis_index("ctx"), lax.axis_index("tp")]).astype(jnp.int32)
+    seg = segment_ids.reshape(1, frames)
+    piece = (3, rows, HEAD_DIM)
+    tall = (frames, HEAD_DIM)
+    w_spec = {0: pl.BlockSpec((width, depth), lambda step, ids: (ids[1], 0))}
+
+    packed = call(
+        functools.partial(pack_kernel, n, HEAD_DIM), "pack", ids, [queries, key_rows, value_rows], [(piece, BF16)] * n
+    )
+    pieces = swap_all(packed, "ctx", n)
+
+    codes = [codebook_ids] + [swap(codebook_ids, "tp", t, i) for i in range(1, t)]
+    found = call(
+        functools.partial(lookup_kernel, t),
+        "lookup",
+        ids,
+        [code_table] + codes,
+        [((books, local, depth), BF16)] * t,
+        in_specs={0: pl.BlockSpec((1, shard_rows, depth), lambda step, ids: (step, 0, 0))},
+        out_specs={i: pl.BlockSpec((1, local, depth), lambda step, ids: (step, 0, 0)) for i in range(t)},
+        grid=(books,),
+    )
+    embedded = sum(x.astype(F32) for x in swap_all(found, "tp", t)).astype(BF16)
+    cotangent = upstream.transpose(1, 0, 2)
+
+    forward = call(
+        functools.partial(forward_kernel, n, rows, window, factor),
+        "attend",
+        ids,
+        [seg] + pieces,
+        [((rows, HEAD_DIM), BF16)] * n + [(tall, BF16), ((1, frames), F32)],
+        [pltpu.VMEM(tall, BF16)] * 3,
+    )
+    out_pieces, out_full, norm = swap_all(forward[:n], "ctx", n), forward[n], forward[n + 1]
+    projected = call(
+        functools.partial(project_kernel, n, t),
+        "project",
+        ids,
+        [input_proj] + out_pieces,
+        [((rows, width), BF16)] + [((local, depth), BF16)] * t,
+        [pltpu.VMEM((rows, depth), BF16)],
+        in_specs=w_spec,
+    )
+    attn_out = projected[0]
+    depth_rows, grad_sum, gain_term = call(
+        functools.partial(depth_kernel, t, books),
+        "depth",
+        ids,
+        [norm_gain.reshape(1, depth), embedded, cotangent] + swap_all(projected[1:], "tp", t),
+        [((books, local, depth), BF16), ((local, depth), BF16), ((1, depth), F32)],
+    )
+    sums = [grad_sum] + [swap(grad_sum, "tp", t, i) for i in range(1, t)]
+    attn_grads = call(
+        functools.partial(grad_attn_kernel, n, t),
+        "grad_attn",
+        ids,
+        [input_proj] + sums,
+        [((rows, depth), BF16)] + [((rows, HEAD_DIM), BF16)] * n,
+        [pltpu.VMEM((rows, width), BF16)],
+        in_specs=w_spec,
+    )
+    grad_pieces = swap_all(attn_grads[1:], "ctx", n)
+    slab = (width, depth // n)
+    proj_terms = call(
+        functools.partial(grad_proj_kernel, n),
+        "grad_proj",
+        ids,
+        [attn_out, attn_grads[0]],
+        [((n // 2,) + slab, BF16)] + [(slab, BF16)] * (n // 2),
+        [pltpu.VMEM((width, depth), BF16)],
+    )
+    other = swap(proj_terms[0], "ctx", n, 1)
+    pair = [(proj_terms[1 + i].astype(F32) + other[i].astype(F32)) for i in range(n // 2)]
+    grad_proj = pair[0]
+    for i in range(1, n // 2):
+        grad_proj = grad_proj + swap(pair[i].astype(BF16), "ctx", n, 2 * i).astype(F32)
+
+    grads = call(
+        functools.partial(backward_kernel, n, rows, window, factor, scale),
+        "attend_grad",
+        ids,
+        [seg, norm, out_full] + pieces + grad_pieces,
+        [(piece, BF16)] * n,
+        [pltpu.VMEM(tall, BF16)] * 5 + [pltpu.VMEM(tall, F32)] * 2,
+    )
+    grad_query, grad_key, grad_value = call(
+        functools.partial(assemble_kernel, n), "assemble", ids, swap_all(grads, "ctx", n), [((rows, width), F32)] * 3
+    )
+    gain = scatter_sum(gain_term.reshape(depth), "ctx", n)
+    grad_gain = scatter_sum(gain, "tp", t)
+    return (depth_rows.transpose(1, 0, 2), grad_query, grad_key, grad_value, grad_proj, grad_gain)
+
+
+def body(n, t, queries, *rest):
+    heads = queries.shape[1] // HEAD_DIM
+    if heads == n and n & (n - 1) == 0 and t & (t - 1) == 0 and n > 1:
+        return heads_body(n, t, queries, *rest)
+    return general_body(queries, *rest)
+
+
+def general_body(
     queries,
     key_rows,
     value_rows,
@@ -220,7 +552,7 @@
 
 def solution(mesh):
     return jax.shard_map(
-        body,
+        functools.partial(body, mesh.shape["ctx"], mesh.shape["tp"]),
         mesh=mesh,
         in_specs=(
             P("ctx", "tp"),

time: 426 us -> 229 us (0.54); the launches traced: 421 us -> 229 us
  local copies, waits for them, and re-layouts: 97.7 us -> 13.7 us
  blocking collectives: 70.1 us -> 0 us
  waiting for transfers between devices: 174 us -> 105 us
  starting transfers between devices: 0.29 us -> 63.7 us
  Pallas kernels: 0 us -> 37.6 us
  matrix products: 33.1 us -> 0 us
  between operations: 14.3 us -> 0.84 us
  loops' own time: 12.4 us -> 0 us
  other arithmetic: 19.2 us -> 7.39 us
    reduce_scatter x4 -> x0, waiting for transfers between devices: 128 us -> none  [the longest x1 55 us: body(): lax.psum_scatter(looked.astype(jnp.bfloat16), 'tp', scatter_dimension=0,...]
    ppermute x0 -> x49, waiting for transfers between devices: none -> 105 us  [swap(): return lax.ppermute(x, axis, [(b, b ^ i) for b in range(count)])]
    ppermute x0 -> x49, starting transfers between devices: none -> 63.7 us  [swap(): return lax.ppermute(x, axis, [(b, b ^ i) for b in range(count)])]
    unnamed x1 -> x0, blocking collectives: 57.3 us -> none
    dynamic_update_slice x12 -> x0, local copies, waits for them, and re-layouts: 46.2 us -> none  [the longest x8 40.1 us: body(): lax.scan(stats_step, (start_top, start_mass), block_list)]
    all_gather x2 -> x0, waiting for transfers between devices: 45.2 us -> none  [the longest x1 45.2 us: body(): lax.all_gather(key_rows, 'ctx', axis=0, tiled=True)]
    pallas_call x0 -> x9, Pallas kernels: none -> 37.6 us  [call(): pl.pallas_call(kernel, name=name, out_shape=[jax.ShapeDtypeStruct(shape,...]
    dot_general x18 -> x0, matrix products: 33.1 us -> none  [the longest x1 7.41 us: body(): jnp.einsum('tcr,crw->tcw', selector, code_table, preferred_element_type=j...]
  transfers between devices with their start and end apart: 7 -> 49, of which waited for: 4 -> 29; matrix products, arithmetic and copies ran while one was open for 28% -> 4% of each run, Pallas kernels for 0% -> 13%
where the time goes in v1:
time: 229 us
  waiting for transfers between devices  105 us (46%)
  starting transfers between devices  63.7 us (28%)
  Pallas kernels  37.6 us (16%)
  local copies, waits for them, and re-layouts  13.7 us (6%)
  other arithmetic  7.39 us (3%)
    ppermute x49, waiting for transfers between devices, swap(): return lax.ppermute(x, axis, [(b, b ^ i) for b in range(count)])  105 us
    ppermute x49, starting transfers between devices, swap(): return lax.ppermute(x, axis, [(b, b ^ i) for b in range(count)])  63.7 us
    pallas_call x9, Pallas kernels, call(): pl.pallas_call(kernel, name=name, out_shape=[jax.ShapeDtypeStruct(shape,...  37.6 us
    unnamed x59, local copies, waits for them, and re-layouts  12.4 us
  transfers between devices with their start and end apart: 49, of which 29 were waited for; matrix products, arithmetic and copies ran while one was open for 4% of the time, Pallas kernels for 13%

profile of v1, /device:TPU:9, one launch (start us, length us, event | category | flops | bytes accessed | tf_op | source)
XLA Modules:
  0.0 228.6 jit_solution(13548966722852670252)
XLA Ops:
  9.9 9.1 %lookup.1 = (bf16[8,64,1024]{2,1,0:T(8,128)(2,1)S(1)}, bf16[8,64,1024]{2,1,0:T(8,128)(2,1)S(1)}, bf16[8,64,1024]{2,1,0:T(8,128)(2,1)S(1)}, bf16[8,64,1024]{2,1,0:T(8,128)(2,1)}) custom-call(s32[2]{0:T(128)S(1)} %pad_add_fusion.ids, bf16[8,512,1024]{2,1,0:T(8,128)(2,1)} %table_ref.1, s32[64,8]{1,0:T(8,128)S(1)} %copy.18.refs_0_, ...), custom_call_target="tpu_custom_call" | custom-call | tf_op jit(solution)/shard_map/lookup/pallas_call | solution.py:34
  19.0 2.2 collective-permute-start.5
  21.6 2.5 %collective-permute-start.8 = (bf16[3,256,128]{2,1,0:T(8,128)(2,1)S(1)}, bf16[3,256,128]{2,1,0:T(8,128)(2,1)S(1)}, u32[]{:S(2)}, u32[]{:S(2)}) collective-permute-start(bf16[3,256,128]{2,1,0:T(8,128)(2,1)S(1)} %get-tuple-element.68), channel_id=1, source_target_pairs={{0,12},{4,8},{8,4},{12,0},{16,28},{20,24},{24,20},{28,16},{1,13},{... | collective-permute-start | bytes 589832 | tf_op jit(solution)/shard_map/ppermute | solution.py:217
  24.2 3.0 %collective-permute-done.7.refs_2_ = bf16[3,256,128]{2,1,0:T(8,128)(2,1)S(1)} collective-permute-done((bf16[3,256,128]{2,1,0:T(8,128)(2,1)S(1)}, bf16[3,256,128]{2,1,0:T(8,128)(2,1)S(1)}, u32[]{:S(2)}, u32[]{:S(2)}) %collective-permute-start.7) | collective-permute-done | bytes 196640 | tf_op jit(solution)/shard_map/ppermute | solution.py:217
  27.1 2.3 %collective-permute-start.9 = (bf16[3,256,128]{2,1,0:T(8,128)(2,1)S(1)}, bf16[3,256,128]{2,1,0:T(8,128)(2,1)S(1)}, u32[]{:S(2)}, u32[]{:S(2)}) collective-permute-start(bf16[3,256,128]{2,1,0:T(8,128)(2,1)S(1)} %get-tuple-element.69), channel_id=1, source_target_pairs={{0,16},{4,20},{8,24},{12,28},{16,0},{20,4},{24,8},{28,12},{1,17},{... | collective-permute-start | bytes 589832 | tf_op jit(solution)/shard_map/ppermute | solution.py:217
  29.5 4.7 %collective-permute-done.8.refs_3_ = bf16[3,256,128]{2,1,0:T(8,128)(2,1)S(1)} collective-permute-done((bf16[3,256,128]{2,1,0:T(8,128)(2,1)S(1)}, bf16[3,256,128]{2,1,0:T(8,128)(2,1)S(1)}, u32[]{:S(2)}, u32[]{:S(2)}) %collective-permute-start.8) | collective-permute-done | bytes 196640 | tf_op jit(solution)/shard_map/ppermute | solution.py:217
  36.6 10.3 %collective-permute-done.10.refs_5_ = bf16[3,256,128]{2,1,0:T(8,128)(2,1)S(1)} collective-permute-done((bf16[3,256,128]{2,1,0:T(8,128)(2,1)S(1)}, bf16[3,256,128]{2,1,0:T(8,128)(2,1)S(1)}, u32[]{:S(2)}, u32[]{:S(2)}) %collective-permute-start.10) | collective-permute-done | bytes 196640 | tf_op jit(solution)/shard_map/ppermute | solution.py:217
  47.0 3.4 %collective-permute-start.12 = (bf16[3,256,128]{2,1,0:T(8,128)(2,1)S(1)}, bf16[3,256,128]{2,1,0:T(8,128)(2,1)S(1)}, u32[]{:S(2)}, u32[]{:S(2)}) collective-permute-start(bf16[3,256,128]{2,1,0:T(8,128)(2,1)S(1)} %get-tuple-element.72), channel_id=1, source_target_pairs={{0,28},{4,24},{8,20},{12,16},{16,12},{20,8},{24,4},{28,0},{1,29},{... | collective-permute-start | bytes 589832 | tf_op jit(solution)/shard_map/ppermute | solution.py:217
  50.4 4.7 %collective-permute-done.11.refs_6_ = bf16[3,256,128]{2,1,0:T(8,128)(2,1)S(1)} collective-permute-done((bf16[3,256,128]{2,1,0:T(8,128)(2,1)S(1)}, bf16[3,256,128]{2,1,0:T(8,128)(2,1)S(1)}, u32[]{:S(2)}, u32[]{:S(2)}) %collective-permute-start.11) | collective-permute-done | bytes 196640 | tf_op jit(solution)/shard_map/ppermute | solution.py:217
  55.0 9.5 %collective-permute-done.12.refs_7_ = bf16[3,256,128]{2,1,0:T(8,128)(2,1)S(1)} collective-permute-done((bf16[3,256,128]{2,1,0:T(8,128)(2,1)S(1)}, bf16[3,256,128]{2,1,0:T(8,128)(2,1)S(1)}, u32[]{:S(2)}, u32[]{:S(2)}) %collective-permute-start.12) | collective-permute-done | bytes 196640 | tf_op jit(solution)/shard_map/ppermute | solution.py:217
  64.5 5.8 %attend.1 = (bf16[256,128]{1,0:T(8,128)(2,1)S(1)}, bf16[256,128]{1,0:T(8,128)(2,1)S(1)}, bf16[256,128]{1,0:T(8,128)(2,1)S(1)}, bf16[256,128]{1,0:T(8,128)(2,1)S(...) custom-call(s32[2]{0:T(128)S(1)} %pad_add_fusion.ids, ...), custom_call_target="tpu_custom_call" | custom-call | tf_op jit(solution)/shard_map/attend/pallas_call | solution.py:34
  75.8 2.2 collective-permute-start.17
  79.4 3.2 %collective-permute-done.17.refs_5_ = bf16[256,128]{1,0:T(8,128)(2,1)S(1)} collective-permute-done((bf16[256,128]{1,0:T(8,128)(2,1)S(1)}, bf16[256,128]{1,0:T(8,128)(2,1)S(1)}, u32[]{:S(2)}, u32[]{:S(2)}) %collective-permute-start.17) | collective-permute-done | bytes 65568 | tf_op jit(solution)/shard_map/ppermute | solution.py:217
  84.5 2.7 %collective-permute-done.19.refs_7_ = bf16[256,128]{1,0:T(8,128)(2,1)S(1)} collective-permute-done((bf16[256,128]{1,0:T(8,128)(2,1)S(1)}, bf16[256,128]{1,0:T(8,128)(2,1)S(1)}, u32[]{:S(2)}, u32[]{:S(2)}) %collective-permute-start.19) | collective-permute-done | bytes 65568 | tf_op jit(solution)/shard_map/ppermute | solution.py:217
  87.2 3.0 %project.1 = (bf16[256,1024]{1,0:T(8,128)(2,1)S(1)}, bf16[64,1024]{1,0:T(8,128)(2,1)S(1)}, bf16[64,1024]{1,0:T(8,128)(2,1)S(1)}, bf16[64,1024]{1,0:T(8,128)(2,1)S(1)}, bf16[64,1024]{1,0:T(8,128)(2,1)S(1)}) custom-call(s32[2]{0:T(128)S(1)} %pad_add_fusion.ids, bf16[4096,1024]{1,0:T(8,128)(2,1)} %w_ref.3, bf16[256,128]{1,0:T(8,128)(2,1)S(1)} %get-tuple-element.73.refs_0_, ...), custom_call_target="tpu_custom_call" | custom-call | tf_op jit(solution)/shard_map/project/pallas_call | solution.py:34
  95.6 2.7 %collective-permute-done.22.refs_3_ = bf16[64,1024]{1,0:T(8,128)(2,1)S(1)} collective-permute-done((bf16[64,1024]{1,0:T(8,128)(2,1)S(1)}, bf16[64,1024]{1,0:T(8,128)(2,1)S(1)}, u32[]{:S(2)}, u32[]{:S(2)}) %collective-permute-start.22) | collective-permute-done | bytes 131104 | tf_op jit(solution)/shard_map/ppermute | solution.py:217
  104.1 2.6 %collective-permute-done.24.refs_2_ = bf16[64,1024]{1,0:T(8,128)(2,1)S(1)} collective-permute-done((bf16[64,1024]{1,0:T(8,128)(2,1)S(1)}, bf16[64,1024]{1,0:T(8,128)(2,1)S(1)}, u32[]{:S(2)}, u32[]{:S(2)}) %collective-permute-start.24) | collective-permute-done | bytes 131104 | tf_op jit(solution)/shard_map/ppermute | solution.py:217
  107.3 3.0 %grad_attn.1 = (bf16[256,1024]{1,0:T(8,128)(2,1)S(1)}, bf16[256,128]{1,0:T(8,128)(2,1)S(1)}, bf16[256,128]{1,0:T(8,128)(2,1)S(1)}, bf16[256,128]{1,0:T(8,128)(2,...) custom-call(s32[2]{0:T(128)S(1)} %pad_add_fusion.ids, ...), custom_call_target="tpu_custom_call" | custom-call | tf_op jit(solution)/shard_map/grad_attn/pallas_call | solution.py:34
  114.7 3.0 %grad_proj.1 = (bf16[4,1024,128]{2,1,0:T(8,128)(2,1)}, bf16[1024,128]{1,0:T(8,128)(2,1)S(1)}, bf16[1024,128]{1,0:T(8,128)(2,1)S(1)}, bf16[1024,128]{1,0:T(8,128)(2,1)S(1)}, bf16[1024,128]{1,0:T(8,128)(2,1)S(1)}) custom-call(s32[2]{0:T(128)S(1)} %pad_add_fusion.ids, bf16[256,1024]{1,0:T(8,128)(2,1)S(1)} %get-tuple-element.108.attn_ref, ...), custom_call_target="tpu_custom_call" | custom-call | tf_op jit(solution)/shard_map/grad_proj/pallas_call | solution.py:34
  118.4 3.0 %collective-permute-start.40 = (bf16[4,1024,128]{2,1,0:T(8,128)(2,1)}, bf16[4,1024,128]{2,1,0:T(8,128)(2,1)}, u32[]{:S(2)}, u32[]{:S(2)}) collective-permute-start(bf16[4,1024,128]{2,1,0:T(8,128)(2,1)} %get-tuple-element.111), channel_id=1, source_target_pairs={{0,4},{4,0},{8,12},{12,8},{16,20},{20,16},{24,28},{28,24},{1,5},{5... | collective-permute-start | bytes 3145736 | tf_op jit(solution)/shard_map/ppermute | solution.py:217
  121.4 4.7 %collective-permute-start.44 = (f32[512]{0:T(512)S(1)}, f32[512]{0:T(512)S(1)}, u32[]{:S(2)}, u32[]{:S(2)}) collective-permute-start(f32[512]{0:T(512)S(1)} %bitcast.36), channel_id=1, source_target_pairs={{0,16},{4,20},{8,24},{12,28},{16,0},{20,4},{24,8},{28,12},{1,17},{... | collective-permute-start | bytes 6152 | tf_op jit(solution)/shard_map/ppermute | solution.py:217
  146.0 4.1 %collective-permute-done.30.refs_13_ = bf16[256,128]{1,0:T(8,128)(2,1)S(1)} collective-permute-done((bf16[256,128]{1,0:T(8,128)(2,1)}, bf16[256,128]{1,0:T(8,128)(2,1)S(1)}, u32[]{:S(2)}, u32[]{:S(2)}) %collective-permute-start.30) | collective-permute-done | bytes 65568 | tf_op jit(solution)/shard_map/ppermute | solution.py:217
  150.1 2.5 %collective-permute-done.31.refs_14_ = bf16[256,128]{1,0:T(8,128)(2,1)S(1)} collective-permute-done((bf16[256,128]{1,0:T(8,128)(2,1)}, bf16[256,128]{1,0:T(8,128)(2,1)S(1)}, u32[]{:S(2)}, u32[]{:S(2)}) %collective-permute-start.31) | collective-permute-done | bytes 65568 | tf_op jit(solution)/shard_map/ppermute | solution.py:217
  155.0 8.3 %attend_grad.1 = (bf16[3,256,128]{2,1,0:T(8,128)(2,1)S(1)}, bf16[3,256,128]{2,1,0:T(8,128)(2,1)S(1)}, bf16[3,256,128]{2,1,0:T(8,128)(2,1)S(1)}, bf16[3,256,128]{...) custom-call(s32[2]{0:T(128)S(1)} %pad_add_fusion.ids, ...), custom_call_target="tpu_custom_call" | custom-call | tf_op jit(solution)/shard_map/attend_grad/pallas_call | solution.py:34
  171.1 3.8 %collective-permute-done.34.refs_2_ = bf16[3,256,128]{2,1,0:T(8,128)(2,1)S(1)} collective-permute-done((bf16[3,256,128]{2,1,0:T(8,128)(2,1)S(1)}, bf16[3,256,128]{2,1,0:T(8,128)(2,1)S(1)}, u32[]{:S(2)}, u32[]{:S(2)}) %collective-permute-start.34) | collective-permute-done | bytes 196640 | tf_op jit(solution)/shard_map/ppermute | solution.py:217
  174.9 2.9 %collective-permute-start.42 = (bf16[1024,128]{1,0:T(8,128)(2,1)}, bf16[1024,128]{1,0:T(8,128)(2,1)}, u32[]{:S(2)}, u32[]{:S(2)}) collective-permute-start(bf16[1024,128]{1,0:T(8,128)(2,1)} %get-tuple-element.124), channel_id=1, source_target_pairs={{0,16},{4,20},{8,24},{12,28},{16,0},{20,4},{24,8},{28,12},{1,17},{... | collective-permute-start | bytes 786440 | tf_op jit(solution)/shard_map/ppermute | solution.py:217
  179.5 2.7 %collective-permute-start.41 = (bf16[1024,128]{1,0:T(8,128)(2,1)}, bf16[1024,128]{1,0:T(8,128)(2,1)}, u32[]{:S(2)}, u32[]{:S(2)}) collective-permute-start(bf16[1024,128]{1,0:T(8,128)(2,1)} %get-tuple-element.122), channel_id=1, source_target_pairs={{0,8},{4,12},{8,0},{12,4},{16,24},{20,28},{24,16},{28,20},{1,9},{5... | collective-permute-start | bytes 786440 | tf_op jit(solution)/shard_map/ppermute | solution.py:217
  184.3 9.0 %collective-permute-done.37.refs_5_ = bf16[3,256,128]{2,1,0:T(8,128)(2,1)S(1)} collective-permute-done((bf16[3,256,128]{2,1,0:T(8,128)(2,1)}, bf16[3,256,128]{2,1,0:T(8,128)(2,1)S(1)}, u32[]{:S(2)}, u32[]{:S(2)}) %collective-permute-start.37) | collective-permute-done | bytes 196640 | tf_op jit(solution)/shard_map/ppermute | solution.py:217
  193.3 3.3 %collective-permute-start.39 = (bf16[3,256,128]{2,1,0:T(8,128)(2,1)S(1)}, bf16[3,256,128]{2,1,0:T(8,128)(2,1)S(1)}, u32[]{:S(2)}, u32[]{:S(2)}) collective-permute-start(bf16[3,256,128]{2,1,0:T(8,128)(2,1)S(1)} %copy-done.13), channel_id=1, source_target_pairs={{0,28},{4,24},{8,20},{12,16},{16,12},{20,8},{24,4},{28,0},{1,29},{... | collective-permute-start | bytes 589832 | tf_op jit(solution)/shard_map/ppermute | solution.py:217
  197.1 21.9 %collective-permute-done.38.refs_6_ = bf16[3,256,128]{2,1,0:T(8,128)(2,1)S(1)} collective-permute-done((bf16[3,256,128]{2,1,0:T(8,128)(2,1)S(1)}, bf16[3,256,128]{2,1,0:T(8,128)(2,1)S(1)}, u32[]{:S(2)}, u32[]{:S(2)}) %collective-permute-start.38) | collective-permute-done | bytes 196640 | tf_op jit(solution)/shard_map/ppermute | solution.py:217
  219.1 4.8 %collective-permute-done.39.refs_7_ = bf16[3,256,128]{2,1,0:T(8,128)(2,1)S(1)} collective-permute-done((bf16[3,256,128]{2,1,0:T(8,128)(2,1)S(1)}, bf16[3,256,128]{2,1,0:T(8,128)(2,1)S(1)}, u32[]{:S(2)}, u32[]{:S(2)}) %collective-permute-start.39) | collective-permute-done | bytes 196640 | tf_op jit(solution)/shard_map/ppermute | solution.py:217
  223.9 2.6 %assemble.1 = (f32[256,1024]{1,0:T(8,128)}, f32[256,1024]{1,0:T(8,128)}, f32[256,1024]{1,0:T(8,128)}) custom-call(s32[2]{0:T(128)S(1)} %pad_add_fusion.ids, bf16[3,256,128]{2,1,0:T(8,128)(2,1)S(1)} %copy-done.7, bf16[3,256,128]{2,1,0:T(8,128)(2,1)S(1)} %collective-permute-done.33.refs_1_, bf16[3,256,128]{2,1,0:T(8,128)(2,1)S(1)} %collective-permute-done.34.refs_2_, ...), custom_call_target="tpu_custom_call" | custom-call | tf_op jit(solution)/shard_map/assemble/pallas_call | solution.py:34
  (148 shorter events, 74.4 us)
Async XLA Ops:
  1.4 8.4 %collective-permute-start = (s32[64,8]{1,0:T(8,128)S(1)}, s32[64,8]{1,0:T(8,128)S(1)}, u32[]{:S(2)}, u32[]{:S(2)}) collective-permute-start(s32[64,8]{1,0:T(8,128)S(1)} %copy.18.refs_0_), channel_id=1, source_target_pairs={{0,1},{1,0},{2,3},{3,2},{4,5},{5,4},{6,7},{7,6},{8,9},{9,8},{10,11... | collective-permute-start | bytes 6152 | tf_op jit(solution)/shard_map/ppermute | solution.py:217
  2.7 7.2 %collective-permute-start.1 = (s32[64,8]{1,0:T(8,128)S(1)}, s32[64,8]{1,0:T(8,128)S(1)}, u32[]{:S(2)}, u32[]{:S(2)}) collective-permute-start(s32[64,8]{1,0:T(8,128)S(1)} %copy.18.refs_0_), channel_id=1, source_target_pairs={{0,2},{1,3},{2,0},{3,1},{4,6},{5,7},{6,4},{7,5},{8,10},{9,11},{10,... | collective-permute-start | bytes 6152 | tf_op jit(solution)/shard_map/ppermute | solution.py:217
  3.9 6.0 %collective-permute-start.2 = (s32[64,8]{1,0:T(8,128)S(1)}, s32[64,8]{1,0:T(8,128)S(1)}, u32[]{:S(2)}, u32[]{:S(2)}) collective-permute-start(s32[64,8]{1,0:T(8,128)S(1)} %copy.18.refs_0_), channel_id=1, source_target_pairs={{0,3},{1,2},{2,1},{3,0},{4,7},{5,6},{6,5},{7,4},{8,11},{9,10},{10,... | collective-permute-start | bytes 6152 | tf_op jit(solution)/shard_map/ppermute | solution.py:217
  8.3 13.4 %collective-permute-start.6 = (bf16[3,256,128]{2,1,0:T(8,128)(2,1)S(1)}, bf16[3,256,128]{2,1,0:T(8,128)(2,1)S(1)}, u32[]{:S(2)}, u32[]{:S(2)}) collective-permute-start(bf16[3,256,128]{2,1,0:T(8,128)(2,1)S(1)} %get-tuple-element.66), channel_id=1, source_target_pairs={{0,4},{4,0},{8,12},{12,8},{16,20},{20,16},{24,28},{28,24},{1,5},{5... | collective-permute-start | bytes 589832 | tf_op jit(solution)/shard_map/ppermute | solution.py:217
  19.0 73.7 %collective-permute-start.5 = (bf16[8,64,1024]{2,1,0:T(8,128)(2,1)}, bf16[8,64,1024]{2,1,0:T(8,128)(2,1)S(1)}, u32[]{:S(2)}, u32[]{:S(2)}) collective-permute-start(bf16[8,64,1024]{2,1,0:T(8,128)(2,1)} %get-tuple-element.64), channel_id=1, source_target_pairs={{0,3},{1,2},{2,1},{3,0},{4,7},{5,6},{6,5},{7,4},{8,11},{9,10},{10,... | collective-permute-start | bytes 3145736 | tf_op jit(solution)/shard_map/ppermute | solution.py:217
  21.1 71.8 %collective-permute-start.4 = (bf16[8,64,1024]{2,1,0:T(8,128)(2,1)S(1)}, bf16[8,64,1024]{2,1,0:T(8,128)(2,1)S(1)}, u32[]{:S(2)}, u32[]{:S(2)}) collective-permute-start(bf16[8,64,1024]{2,1,0:T(8,128)(2,1)S(1)} %get-tuple-element.63), channel_id=1, source_target_pairs={{0,2},{1,3},{2,0},{3,1},{4,6},{5,7},{6,4},{7,5},{8,10},{9,11},{10,... | collective-permute-start | bytes 3145736 | tf_op jit(solution)/shard_map/ppermute | solution.py:217
  21.4 71.6 %collective-permute-start.3 = (bf16[8,64,1024]{2,1,0:T(8,128)(2,1)S(1)}, bf16[8,64,1024]{2,1,0:T(8,128)(2,1)S(1)}, u32[]{:S(2)}, u32[]{:S(2)}) collective-permute-start(bf16[8,64,1024]{2,1,0:T(8,128)(2,1)S(1)} %get-tuple-element.62), channel_id=1, source_target_pairs={{0,1},{1,0},{2,3},{3,2},{4,5},{5,4},{6,7},{7,6},{8,9},{9,8},{10,11... | collective-permute-start | bytes 3145736 | tf_op jit(solution)/shard_map/ppermute | solution.py:217
  21.6 12.5 %collective-permute-start.8 = (bf16[3,256,128]{2,1,0:T(8,128)(2,1)S(1)}, bf16[3,256,128]{2,1,0:T(8,128)(2,1)S(1)}, u32[]{:S(2)}, u32[]{:S(2)}) collective-permute-start(bf16[3,256,128]{2,1,0:T(8,128)(2,1)S(1)} %get-tuple-element.68), channel_id=1, source_target_pairs={{0,12},{4,8},{8,4},{12,0},{16,28},{20,24},{24,20},{28,16},{1,13},{... | collective-permute-start | bytes 589832 | tf_op jit(solution)/shard_map/ppermute | solution.py:217
  27.1 9.5 %collective-permute-start.9 = (bf16[3,256,128]{2,1,0:T(8,128)(2,1)S(1)}, bf16[3,256,128]{2,1,0:T(8,128)(2,1)S(1)}, u32[]{:S(2)}, u32[]{:S(2)}) collective-permute-start(bf16[3,256,128]{2,1,0:T(8,128)(2,1)S(1)} %get-tuple-element.69), channel_id=1, source_target_pairs={{0,16},{4,20},{8,24},{12,28},{16,0},{20,4},{24,8},{28,12},{1,17},{... | collective-permute-start | bytes 589832 | tf_op jit(solution)/shard_map/ppermute | solution.py:217
  34.2 12.8 %collective-permute-start.10 = (bf16[3,256,128]{2,1,0:T(8,128)(2,1)S(1)}, bf16[3,256,128]{2,1,0:T(8,128)(2,1)S(1)}, u32[]{:S(2)}, u32[]{:S(2)}) collective-permute-start(bf16[3,256,128]{2,1,0:T(8,128)(2,1)S(1)} %get-tuple-element.70), channel_id=1, source_target_pairs={{0,20},{4,16},{8,28},{12,24},{16,4},{20,0},{24,12},{28,8},{1,21},{... | collective-permute-start | bytes 589832 | tf_op jit(solution)/shard_map/ppermute | solution.py:217
  36.6 18.4 %collective-permute-start.11 = (bf16[3,256,128]{2,1,0:T(8,128)(2,1)S(1)}, bf16[3,256,128]{2,1,0:T(8,128)(2,1)S(1)}, u32[]{:S(2)}, u32[]{:S(2)}) collective-permute-start(bf16[3,256,128]{2,1,0:T(8,128)(2,1)S(1)} %get-tuple-element.71), channel_id=1, source_target_pairs={{0,24},{4,28},{8,16},{12,20},{16,8},{20,12},{24,0},{28,4},{1,25},{... | collective-permute-start | bytes 589832 | tf_op jit(solution)/shard_map/ppermute | solution.py:217
  47.0 17.5 %collective-permute-start.12 = (bf16[3,256,128]{2,1,0:T(8,128)(2,1)S(1)}, bf16[3,256,128]{2,1,0:T(8,128)(2,1)S(1)}, u32[]{:S(2)}, u32[]{:S(2)}) collective-permute-start(bf16[3,256,128]{2,1,0:T(8,128)(2,1)S(1)} %get-tuple-element.72), channel_id=1, source_target_pairs={{0,28},{4,24},{8,20},{12,16},{16,12},{20,8},{24,4},{28,0},{1,29},{... | collective-permute-start | bytes 589832 | tf_op jit(solution)/shard_map/ppermute | solution.py:217
  75.8 6.7 %collective-permute-start.17 = (bf16[256,128]{1,0:T(8,128)(2,1)S(1)}, bf16[256,128]{1,0:T(8,128)(2,1)S(1)}, u32[]{:S(2)}, u32[]{:S(2)}) collective-permute-start(bf16[256,128]{1,0:T(8,128)(2,1)S(1)} %get-tuple-element.78), channel_id=1, source_target_pairs={{0,20},{4,16},{8,28},{12,24},{16,4},{20,0},{24,12},{28,8},{1,21},{... | collective-permute-start | bytes 196616 | tf_op jit(solution)/shard_map/ppermute | solution.py:217
  78.0 6.5 %collective-permute-start.18 = (bf16[256,128]{1,0:T(8,128)(2,1)S(1)}, bf16[256,128]{1,0:T(8,128)(2,1)S(1)}, u32[]{:S(2)}, u32[]{:S(2)}) collective-permute-start(bf16[256,128]{1,0:T(8,128)(2,1)S(1)} %get-tuple-element.79), channel_id=1, source_target_pairs={{0,24},{4,28},{8,16},{12,20},{16,8},{20,12},{24,0},{28,4},{1,25},{... | collective-permute-start | bytes 196616 | tf_op jit(solution)/shard_map/ppermute | solution.py:217
  118.4 47.5 %collective-permute-start.40 = (bf16[4,1024,128]{2,1,0:T(8,128)(2,1)}, bf16[4,1024,128]{2,1,0:T(8,128)(2,1)}, u32[]{:S(2)}, u32[]{:S(2)}) collective-permute-start(bf16[4,1024,128]{2,1,0:T(8,128)(2,1)} %get-tuple-element.111), channel_id=1, source_target_pairs={{0,4},{4,0},{8,12},{12,8},{16,20},{20,16},{24,28},{28,24},{1,5},{5... | collective-permute-start | bytes 3145736 | tf_op jit(solution)/shard_map/ppermute | solution.py:217
  132.5 8.9 %collective-permute-start.26 = (bf16[256,128]{1,0:T(8,128)(2,1)}, bf16[256,128]{1,0:T(8,128)(2,1)S(1)}, u32[]{:S(2)}, u32[]{:S(2)}) collective-permute-start(bf16[256,128]{1,0:T(8,128)(2,1)} %copy-done.22), channel_id=1, source_target_pairs={{0,4},{4,0},{8,12},{12,8},{16,20},{20,16},{24,28},{28,24},{1,5},{5... | collective-permute-start | bytes 196616 | tf_op jit(solution)/shard_map/ppermute | solution.py:217
  132.5 10.6 %collective-permute-start.27 = (bf16[256,128]{1,0:T(8,128)(2,1)}, bf16[256,128]{1,0:T(8,128)(2,1)}, u32[]{:S(2)}, u32[]{:S(2)}) collective-permute-start(bf16[256,128]{1,0:T(8,128)(2,1)} %copy-done.21), channel_id=1, source_target_pairs={{0,8},{4,12},{8,0},{12,4},{16,24},{20,28},{24,16},{28,20},{1,9},{5... | collective-permute-start | bytes 196616 | tf_op jit(solution)/shard_map/ppermute | solution.py:217
  134.3 9.8 %collective-permute-start.28 = (bf16[256,128]{1,0:T(8,128)(2,1)}, bf16[256,128]{1,0:T(8,128)(2,1)}, u32[]{:S(2)}, u32[]{:S(2)}) collective-permute-start(bf16[256,128]{1,0:T(8,128)(2,1)} %copy-done.20), channel_id=1, source_target_pairs={{0,12},{4,8},{8,4},{12,0},{16,28},{20,24},{24,20},{28,16},{1,13},{... | collective-permute-start | bytes 196616 | tf_op jit(solution)/shard_map/ppermute | solution.py:217
  141.4 8.7 %collective-permute-start.30 = (bf16[256,128]{1,0:T(8,128)(2,1)}, bf16[256,128]{1,0:T(8,128)(2,1)S(1)}, u32[]{:S(2)}, u32[]{:S(2)}) collective-permute-start(bf16[256,128]{1,0:T(8,128)(2,1)} %copy-done.18), channel_id=1, source_target_pairs={{0,20},{4,16},{8,28},{12,24},{16,4},{20,0},{24,12},{28,8},{1,21},{... | collective-permute-start | bytes 196616 | tf_op jit(solution)/shard_map/ppermute | solution.py:217
  143.1 9.6 %collective-permute-start.31 = (bf16[256,128]{1,0:T(8,128)(2,1)}, bf16[256,128]{1,0:T(8,128)(2,1)S(1)}, u32[]{:S(2)}, u32[]{:S(2)}) collective-permute-start(bf16[256,128]{1,0:T(8,128)(2,1)} %copy-done.17), channel_id=1, source_target_pairs={{0,24},{4,28},{8,16},{12,20},{16,8},{20,12},{24,0},{28,4},{1,25},{... | collective-permute-start | bytes 196616 | tf_op jit(solution)/shard_map/ppermute | solution.py:217
  144.0 10.2 %collective-permute-start.32 = (bf16[256,128]{1,0:T(8,128)(2,1)}, bf16[256,128]{1,0:T(8,128)(2,1)S(1)}, u32[]{:S(2)}, u32[]{:S(2)}) collective-permute-start(bf16[256,128]{1,0:T(8,128)(2,1)} %copy-done.16), channel_id=1, source_target_pairs={{0,28},{4,24},{8,20},{12,16},{16,12},{20,8},{24,4},{28,0},{1,29},{... | collective-permute-start | bytes 196616 | tf_op jit(solution)/shard_map/ppermute | solution.py:217
  145.1 20.4 %collective-permute-start.48 = (f32[32]{0:T(128)S(1)}, f32[32]{0:T(128)S(1)}, u32[]{:S(2)}, u32[]{:S(2)}) collective-permute-start(f32[32]{0:T(128)S(1)} %dynamic_slice.45), channel_id=1, source_target_pairs={{0,1},{1,0},{2,3},{3,2},{4,5},{5,4},{6,7},{7,6},{8,9},{9,8},{10,11... | collective-permute-start | bytes 392 | tf_op jit(solution)/shard_map/ppermute | solution.py:217
  163.3 6.8 %collective-permute-start.33 = (bf16[3,256,128]{2,1,0:T(8,128)(2,1)S(1)}, bf16[3,256,128]{2,1,0:T(8,128)(2,1)S(1)}, u32[]{:S(2)}, u32[]{:S(2)}) collective-permute-start(bf16[3,256,128]{2,1,0:T(8,128)(2,1)S(1)} %get-tuple-element.98), channel_id=1, source_target_pairs={{0,4},{4,0},{8,12},{12,8},{16,20},{20,16},{24,28},{28,24},{1,5},{5... | collective-permute-start | bytes 589832 | tf_op jit(solution)/shard_map/ppermute | solution.py:217
  163.5 11.4 %collective-permute-start.34 = (bf16[3,256,128]{2,1,0:T(8,128)(2,1)S(1)}, bf16[3,256,128]{2,1,0:T(8,128)(2,1)S(1)}, u32[]{:S(2)}, u32[]{:S(2)}) collective-permute-start(bf16[3,256,128]{2,1,0:T(8,128)(2,1)S(1)} %get-tuple-element.99), channel_id=1, source_target_pairs={{0,8},{4,12},{8,0},{12,4},{16,24},{20,28},{24,16},{28,20},{1,9},{5... | collective-permute-start | bytes 589832 | tf_op jit(solution)/shard_map/ppermute | solution.py:217
  163.5 16.0 %collective-permute-start.35 = (bf16[3,256,128]{2,1,0:T(8,128)(2,1)S(1)}, bf16[3,256,128]{2,1,0:T(8,128)(2,1)S(1)}, u32[]{:S(2)}, u32[]{:S(2)}) collective-permute-start(bf16[3,256,128]{2,1,0:T(8,128)(2,1)S(1)} %get-tuple-element.100), channel_id=1, source_target_pairs={{0,12},{4,8},{8,4},{12,0},{16,28},{20,24},{24,20},{28,16},{1,13},{... | collective-permute-start | bytes 589832 | tf_op jit(solution)/shard_map/ppermute | solution.py:217
  165.5 18.3 %collective-permute-start.36 = (bf16[3,256,128]{2,1,0:T(8,128)(2,1)}, bf16[3,256,128]{2,1,0:T(8,128)(2,1)S(1)}, u32[]{:S(2)}, u32[]{:S(2)}) collective-permute-start(bf16[3,256,128]{2,1,0:T(8,128)(2,1)} %get-tuple-element.101), channel_id=1, source_target_pairs={{0,16},{4,20},{8,24},{12,28},{16,0},{20,4},{24,8},{28,12},{1,17},{... | collective-permute-start | bytes 589832 | tf_op jit(solution)/shard_map/ppermute | solution.py:217
  165.9 27.4 %collective-permute-start.37 = (bf16[3,256,128]{2,1,0:T(8,128)(2,1)}, bf16[3,256,128]{2,1,0:T(8,128)(2,1)S(1)}, u32[]{:S(2)}, u32[]{:S(2)}) collective-permute-start(bf16[3,256,128]{2,1,0:T(8,128)(2,1)} %get-tuple-element.102), channel_id=1, source_target_pairs={{0,20},{4,16},{8,28},{12,24},{16,4},{20,0},{24,12},{28,8},{1,21},{... | collective-permute-start | bytes 589832 | tf_op jit(solution)/shard_map/ppermute | solution.py:217
  170.1 56.4 %collective-permute-start.43 = (bf16[1024,128]{1,0:T(8,128)(2,1)}, bf16[1024,128]{1,0:T(8,128)(2,1)}, u32[]{:S(2)}, u32[]{:S(2)}) collective-permute-start(bf16[1024,128]{1,0:T(8,128)(2,1)} %get-tuple-element.123), channel_id=1, source_target_pairs={{0,24},{4,28},{8,16},{12,20},{16,8},{20,12},{24,0},{28,4},{1,25},{... | collective-permute-start | bytes 786440 | tf_op jit(solution)/shard_map/ppermute | solution.py:217
  174.9 51.6 %collective-permute-start.42 = (bf16[1024,128]{1,0:T(8,128)(2,1)}, bf16[1024,128]{1,0:T(8,128)(2,1)}, u32[]{:S(2)}, u32[]{:S(2)}) collective-permute-start(bf16[1024,128]{1,0:T(8,128)(2,1)} %get-tuple-element.124), channel_id=1, source_target_pairs={{0,16},{4,20},{8,24},{12,28},{16,0},{20,4},{24,8},{28,12},{1,17},{... | collective-permute-start | bytes 786440 | tf_op jit(solution)/shard_map/ppermute | solution.py:217
  179.5 46.9 %collective-permute-start.41 = (bf16[1024,128]{1,0:T(8,128)(2,1)}, bf16[1024,128]{1,0:T(8,128)(2,1)}, u32[]{:S(2)}, u32[]{:S(2)}) collective-permute-start(bf16[1024,128]{1,0:T(8,128)(2,1)} %get-tuple-element.122), channel_id=1, source_target_pairs={{0,8},{4,12},{8,0},{12,4},{16,24},{20,28},{24,16},{28,20},{1,9},{5... | collective-permute-start | bytes 786440 | tf_op jit(solution)/shard_map/ppermute | solution.py:217
  183.8 35.3 %collective-permute-start.38 = (bf16[3,256,128]{2,1,0:T(8,128)(2,1)S(1)}, bf16[3,256,128]{2,1,0:T(8,128)(2,1)S(1)}, u32[]{:S(2)}, u32[]{:S(2)}) collective-permute-start(bf16[3,256,128]{2,1,0:T(8,128)(2,1)S(1)} %copy-done.15), channel_id=1, source_target_pairs={{0,24},{4,28},{8,16},{12,20},{16,8},{20,12},{24,0},{28,4},{1,25},{... | collective-permute-start | bytes 589832 | tf_op jit(solution)/shard_map/ppermute | solution.py:217
  193.3 30.6 %collective-permute-start.39 = (bf16[3,256,128]{2,1,0:T(8,128)(2,1)S(1)}, bf16[3,256,128]{2,1,0:T(8,128)(2,1)S(1)}, u32[]{:S(2)}, u32[]{:S(2)}) collective-permute-start(bf16[3,256,128]{2,1,0:T(8,128)(2,1)S(1)} %copy-done.13), channel_id=1, source_target_pairs={{0,28},{4,24},{8,20},{12,16},{16,12},{20,8},{24,4},{28,0},{1,29},{... | collective-permute-start | bytes 589832 | tf_op jit(solution)/shard_map/ppermute | solution.py:217
  (45 other events, 420.5 us)

commit v2 on v1

--- a/solution.py
+++ b/solution.py
@@ -1,4 +1,5 @@
 import functools
+import math
 
 import jax
 import jax.numpy as jnp
@@ -23,7 +24,7 @@
     return lax.dot_general(a, b, (((a_dim,), (b_dim,)), ((), ())), preferred_element_type=F32)
 
 
-def call(kernel, name, ids, inputs, out_shapes, scratch=(), in_specs=None, out_specs=None, grid=(1,)):
+def call(kernel, name, ids, inputs, out_shapes, scratch=(), in_specs=None, out_specs=None, grid=(1,), flops=0, extra=0, skip=0):
     def whole(shape):
         return pl.BlockSpec(shape, lambda step, ids: (0,) * len(shape))
 
@@ -43,6 +44,11 @@
             scratch_shapes=list(scratch),
         ),
         compiler_params=pltpu.CompilerParams(vmem_limit_bytes=VMEM_BYTES),
+        cost_estimate=pl.CostEstimate(
+            flops=flops,
+            transcendentals=0,
+            bytes_accessed=extra + sum(x.size * x.dtype.itemsize for x in inputs[skip:]) + sum(math.prod(o[0]) * 2 for o in out_shapes),
+        ),
     )(ids, *inputs)
 
 
@@ -50,12 +56,17 @@
     return pl.multiple_of(index * width, width)
 
 
-def pack_kernel(n, width, ids, q_ref, k_ref, v_ref, *outs):
+def pack_kernel(n, width, ids, q_ref, k_ref, v_ref, *refs):
+    outs, sem = refs[:n], refs[n]
     me = ids[0]
+    copies = []
     for i in range(n):
         columns = pl.ds(offset(me ^ i, width), width)
         for part, ref in enumerate((q_ref, k_ref, v_ref)):
-            outs[i][part] = ref[:, columns]
+            copies.append(pltpu.make_async_copy(ref.at[:, columns], outs[i].at[part], sem.at[3 * i + part]))
+            copies[-1].start()
+    for copy in copies:
+        copy.wait()
 
 
 def segment_starts(seg):
@@ -73,8 +84,8 @@
 
 
 def forward_kernel(n, rows, window, factor, ids, seg_ref, *refs):
-    pieces, outs = refs[:n], refs[n : 2 * n]
-    out_ref, norm_ref, q_s, k_s, v_s = refs[2 * n :]
+    pieces = refs[:n]
+    out_ref, norm_ref, q_s, k_s, v_s = refs[n:]
     me = ids[0]
     for i in range(n):
         place = pl.ds(offset(me ^ i, rows), rows)
@@ -93,20 +104,12 @@
         mixed = dot(v_s[low : low + count, :], mass.astype(BF16), 0, 0) / total
         out_ref[first : first + rows, :] = mixed.T.astype(BF16)
         norm_ref[:, first : first + rows] = top + jnp.log2(total)
-    for i in range(n):
-        outs[i][...] = out_ref[pl.ds(offset(me ^ i, rows), rows), :]
-
-
-def backward_kernel(n, rows, window, factor, scale, ids, seg_ref, norm_ref, out_ref, *refs):
-    pieces, grads, outs = refs[:n], refs[n : 2 * n], refs[2 * n : 3 * n]
-    q_s, k_s, v_s, g_s, dq_s, dk_s, dv_s = refs[3 * n :]
+
+
+def backward_kernel(n, rows, window, factor, scale, ids, seg_ref, norm_ref, out_ref, q_s, k_s, v_s, g_s, *refs):
+    outs = refs[:n]
+    dq_s, dk_s, dv_s = refs[n:]
     me = ids[0]
-    for i in range(n):
-        place = pl.ds(offset(me ^ i, rows), rows)
-        q_s[place, :] = pieces[i][0]
-        k_s[place, :] = pieces[i][1]
-        v_s[place, :] = pieces[i][2]
-        g_s[place, :] = grads[i][...]
     starts = segment_starts(seg_ref[...])
     for block in range(n):
         first, low = block * rows, max(0, block - window) * rows
@@ -132,12 +135,11 @@
         outs[i][2] = dv_s[place, :].astype(BF16)
 
 
-def project_kernel(n, t, ids, w_ref, *refs):
-    pieces, attn_ref, outs, total = refs[:n], refs[n], refs[n + 1 : n + 1 + t], refs[n + 1 + t]
-    me, shard = ids[0], ids[1]
-    width = pieces[0].shape[1]
-    for i in range(n):
-        attn_ref[:, pl.ds(offset(me ^ i, width), width)] = pieces[i][...]
+def project_kernel(n, t, ids, w_ref, heads_ref, *refs):
+    attn_ref, outs, total = refs[0], refs[1 : 1 + t], refs[1 + t]
+    shard = ids[1]
+    for i in range(n):
+        attn_ref[:, i * HEAD_DIM : (i + 1) * HEAD_DIM] = heads_ref[i]
     total[...] = dot(attn_ref[...], w_ref[...], 1, 0).astype(BF16)
     rows = outs[0].shape[0]
     for i in range(t):
@@ -161,7 +163,7 @@
 
 def depth_kernel(t, books, ids, gain_ref, embed_ref, up_ref, *refs):
     parts = refs[:t]
-    depth_ref, sum_ref, gain_out_ref = refs[t:]
+    depth_ref, sum_ref = refs[t:]
     projected = parts[0][...].astype(F32)
     for i in range(1, t):
         projected = projected + parts[i][...].astype(F32)
@@ -177,30 +179,34 @@
         gain_sum = gain_sum + cotangent * normed
         grad = cotangent * gain
         grad_sum = grad_sum + inverse * (grad - normed * jnp.mean(grad * normed, axis=1, keepdims=True))
-    sum_ref[...] = grad_sum.astype(BF16)
-    gain_out_ref[...] = jnp.sum(gain_sum, axis=0, keepdims=True)
-
-
-def grad_attn_kernel(n, t, ids, w_ref, *refs):
-    parts, sum_ref, outs, total = refs[:t], refs[t], refs[t + 1 : t + 1 + n], refs[t + 1 + n]
+    rows = grad_sum.shape[0]
+    sum_ref[:rows, :] = grad_sum.astype(BF16)
+    sum_ref[rows:, :] = two_parts(jnp.sum(gain_sum, axis=0, keepdims=True), 0, sum_ref.shape[0] - rows)
+
+
+def two_parts(row, slot, count):
+    high = row.astype(BF16).astype(F32)
+    place = lax.broadcasted_iota(jnp.int32, (count, row.shape[1]), 0)
+    return jnp.where(place == 2 * slot, high, jnp.where(place == 2 * slot + 1, row - high, 0.0)).astype(BF16)
+
+
+def grad_attn_kernel(n, t, ids, w_ref, attn_ref, *refs):
+    parts, out_ref, proj_ref, sum_s = refs[:t], refs[t], refs[t + 1], refs[t + 2]
     me, shard = ids[0], ids[1]
-    rows, width = parts[0].shape[0], outs[0].shape[1]
+    rows = sum_s.shape[0] // t
+    gain = jnp.zeros((1, sum_s.shape[1]), F32)
     for i in range(t):
-        sum_ref[pl.ds(offset(shard ^ i, rows), rows), :] = parts[i][...]
-    total[...] = dot(sum_ref[...], w_ref[...], 1, 1).astype(BF16)
-    for i in range(n):
-        outs[i][...] = total[:, pl.ds(offset(me ^ i, width), width)]
-
-
-def grad_proj_kernel(n, ids, attn_ref, sum_ref, send_ref, *refs):
-    keeps, total = refs[: n // 2], refs[n // 2]
-    me = ids[0]
-    width = keeps[0].shape[1]
-    total[...] = dot(attn_ref[...], sum_ref[...], 0, 0).astype(BF16)
-    for i in range(n // 2):
-        mine = me ^ (2 * i)
-        keeps[i][...] = total[:, pl.ds(offset(mine, width), width)]
-        send_ref[i] = total[:, pl.ds(offset(mine ^ 1, width), width)]
+        sum_s[pl.ds(offset(shard ^ i, rows), rows), :] = parts[i][:rows, :]
+        gain = gain + jnp.sum(parts[i][rows:, :].astype(F32), axis=0, keepdims=True)
+    grad = dot(sum_s[...], w_ref[...], 1, 1).astype(BF16)
+    for i in range(n):
+        out_ref[i] = grad[:, i * HEAD_DIM : (i + 1) * HEAD_DIM]
+    term = dot(attn_ref[...], sum_s[...], 0, 0).astype(BF16)
+    tail = two_parts(gain, me, 2 * n)
+    width, columns = term.shape[0], proj_ref.shape[2]
+    for i in range(n):
+        proj_ref[i, :width, :] = term[:, i * columns : (i + 1) * columns]
+        proj_ref[i, width:, :] = tail[:, i * columns : (i + 1) * columns]
 
 
 def assemble_kernel(n, ids, *refs):
@@ -219,19 +225,6 @@
 
 def swap_all(parts, axis, count):
     return [parts[0]] + [swap(parts[i], axis, count, i) for i in range(1, count)]
-
-
-def scatter_sum(x, axis, count):
-    index = lax.axis_index(axis)
-    step = count // 2
-    while step:
-        half = x.shape[0] // 2
-        bit = (index // step) % 2
-        kept = lax.dynamic_slice_in_dim(x, bit * half, half, 0)
-        sent = lax.dynamic_slice_in_dim(x, (1 - bit) * half, half, 0)
-        x = kept + swap(sent, axis, count, step)
-        step //= 2
-    return x
 
 
 def heads_body(n, t, queries, key_rows, value_rows, segment_ids, codebook_ids, code_table, input_proj, norm_gain, upstream):
@@ -248,8 +241,16 @@
     tall = (frames, HEAD_DIM)
     w_spec = {0: pl.BlockSpec((width, depth), lambda step, ids: (ids[1], 0))}
 
+    raw = pl.BlockSpec(memory_space=pl.ANY)
     packed = call(
-        functools.partial(pack_kernel, n, HEAD_DIM), "pack", ids, [queries, key_rows, value_rows], [(piece, BF16)] * n
+        functools.partial(pack_kernel, n, HEAD_DIM),
+        "pack",
+        ids,
+        [queries, key_rows, value_rows],
+        [(piece, BF16)] * n,
+        [pltpu.SemaphoreType.DMA((3 * n,))],
+        in_specs={i: raw for i in range(3)},
+        out_specs={i: raw for i in range(n)},
     )
     pieces = swap_all(packed, "ctx", n)
 
@@ -263,75 +264,75 @@
         in_specs={0: pl.BlockSpec((1, shard_rows, depth), lambda step, ids: (step, 0, 0))},
         out_specs={i: pl.BlockSpec((1, local, depth), lambda step, ids: (step, 0, 0)) for i in range(t)},
         grid=(books,),
+        flops=2 * books * t * local * shard_rows * depth,
     )
     embedded = sum(x.astype(F32) for x in swap_all(found, "tp", t)).astype(BF16)
     cotangent = upstream.transpose(1, 0, 2)
 
-    forward = call(
+    pair_flops = 4 * frames * (window + 1) * rows * HEAD_DIM
+    out_full, norm, query, key, value = call(
         functools.partial(forward_kernel, n, rows, window, factor),
         "attend",
         ids,
         [seg] + pieces,
-        [((rows, HEAD_DIM), BF16)] * n + [(tall, BF16), ((1, frames), F32)],
-        [pltpu.VMEM(tall, BF16)] * 3,
-    )
-    out_pieces, out_full, norm = swap_all(forward[:n], "ctx", n), forward[n], forward[n + 1]
+        [(tall, BF16), ((1, frames), F32)] + [(tall, BF16)] * 3,
+        flops=pair_flops,
+    )
+    out_heads = lax.all_to_all(out_full.reshape(n, rows, HEAD_DIM), "ctx", 0, 0, tiled=True)
     projected = call(
         functools.partial(project_kernel, n, t),
         "project",
         ids,
-        [input_proj] + out_pieces,
+        [input_proj, out_heads],
         [((rows, width), BF16)] + [((local, depth), BF16)] * t,
         [pltpu.VMEM((rows, depth), BF16)],
         in_specs=w_spec,
+        flops=2 * rows * width * depth,
+        extra=2 * width * depth,
+        skip=1,
     )
     attn_out = projected[0]
-    depth_rows, grad_sum, gain_term = call(
+    extra_rows = 16
+    depth_rows, grad_sum = call(
         functools.partial(depth_kernel, t, books),
         "depth",
         ids,
         [norm_gain.reshape(1, depth), embedded, cotangent] + swap_all(projected[1:], "tp", t),
-        [((books, local, depth), BF16), ((local, depth), BF16), ((1, depth), F32)],
+        [((books, local, depth), BF16), ((local + extra_rows, depth), BF16)],
     )
     sums = [grad_sum] + [swap(grad_sum, "tp", t, i) for i in range(1, t)]
-    attn_grads = call(
+    grad_heads, proj_term = call(
         functools.partial(grad_attn_kernel, n, t),
         "grad_attn",
         ids,
-        [input_proj] + sums,
-        [((rows, depth), BF16)] + [((rows, HEAD_DIM), BF16)] * n,
-        [pltpu.VMEM((rows, width), BF16)],
+        [input_proj, attn_out] + sums,
+        [((n, rows, HEAD_DIM), BF16), ((n, width + 2 * n, depth // n), BF16)],
+        [pltpu.VMEM((rows, depth), BF16)],
         in_specs=w_spec,
-    )
-    grad_pieces = swap_all(attn_grads[1:], "ctx", n)
-    slab = (width, depth // n)
-    proj_terms = call(
-        functools.partial(grad_proj_kernel, n),
-        "grad_proj",
-        ids,
-        [attn_out, attn_grads[0]],
-        [((n // 2,) + slab, BF16)] + [(slab, BF16)] * (n // 2),
-        [pltpu.VMEM((width, depth), BF16)],
-    )
-    other = swap(proj_terms[0], "ctx", n, 1)
-    pair = [(proj_terms[1 + i].astype(F32) + other[i].astype(F32)) for i in range(n // 2)]
-    grad_proj = pair[0]
-    for i in range(1, n // 2):
-        grad_proj = grad_proj + swap(pair[i].astype(BF16), "ctx", n, 2 * i).astype(F32)
-
+        flops=4 * rows * width * depth,
+        extra=2 * width * depth,
+        skip=1,
+    )
+    proj_sum = lax.psum_scatter(
+        proj_term.reshape(n * (width + 2 * n), depth // n), "ctx", scatter_dimension=0, tiled=True
+    )
+    grad_full = lax.all_to_all(grad_heads, "ctx", 0, 0, tiled=True).reshape(tall)
     grads = call(
         functools.partial(backward_kernel, n, rows, window, factor, scale),
         "attend_grad",
         ids,
-        [seg, norm, out_full] + pieces + grad_pieces,
+        [seg, norm, out_full, query, key, value, grad_full],
         [(piece, BF16)] * n,
-        [pltpu.VMEM(tall, BF16)] * 5 + [pltpu.VMEM(tall, F32)] * 2,
+        [pltpu.VMEM(tall, BF16)] + [pltpu.VMEM(tall, F32)] * 2,
+        flops=5 * pair_flops // 2,
     )
     grad_query, grad_key, grad_value = call(
         functools.partial(assemble_kernel, n), "assemble", ids, swap_all(grads, "ctx", n), [((rows, width), F32)] * 3
     )
-    gain = scatter_sum(gain_term.reshape(depth), "ctx", n)
-    grad_gain = scatter_sum(gain, "tp", t)
+    grad_proj = proj_sum[:width].astype(F32)
+    gain = jnp.sum(proj_sum[width:].astype(F32), axis=0)
+    part = depth // (n * t)
+    grad_gain = lax.dynamic_slice_in_dim(gain, lax.axis_index("tp") * part, part, 0)
     return (depth_rows.transpose(1, 0, 2), grad_query, grad_key, grad_value, grad_proj, grad_gain)
 
 

time: 229 us -> 200 us (0.87)
  waiting for transfers between devices: 105 us -> 67.3 us
  starting transfers between devices: 63.7 us -> 36 us
  blocking collectives: 0 us -> 27.7 us
  between operations: 0.84 us -> 14.1 us
  local copies, waits for them, and re-layouts: 13.7 us -> 11.3 us
    ppermute x49 -> x26, waiting for transfers between devices: 105 us -> 57.2 us  [swap(): return lax.ppermute(x, axis, [(b, b ^ i) for b in range(count)])]
    ppermute x49 -> x26, starting transfers between devices: 63.7 us -> 30.8 us  [swap(): return lax.ppermute(x, axis, [(b, b ^ i) for b in range(count)])]
    all_to_all x0 -> x1, blocking collectives: none -> 27.7 us  [heads_body(): lax.all_to_all(grad_heads, 'ctx', 0, 0, tiled=True).reshape(tall)]
    all_to_all x0 -> x1, waiting for transfers between devices: none -> 10 us  [heads_body(): lax.all_to_all(out_full.reshape(n, rows, HEAD_DIM), 'ctx', 0, 0, tiled=True)]
    all_to_all x0 -> x1, starting transfers between devices: none -> 5.19 us  [heads_body(): lax.all_to_all(out_full.reshape(n, rows, HEAD_DIM), 'ctx', 0, 0, tiled=True)]
    add x6 -> x0, other arithmetic: 4.23 us -> none  [the longest x1 2.14 us: heads_body(): grad_proj + swap(pair[i].astype(BF16), 'ctx', n, 2 * i).astype(F32)]
    unnamed x59 -> x25, local copies, waits for them, and re-layouts: 12.4 us -> 10.7 us
    pallas_call x9 -> x8, Pallas kernels: 37.6 us -> 37.6 us  [call(): pl.pallas_call(kernel, name=name, out_shape=[jax.ShapeDtypeStruct(shape,...]
  transfers between devices with their start and end apart: 49 -> 28, of which waited for: 29 -> 14; matrix products, arithmetic and copies ran while one was open for 4% -> 3% of each run, Pallas kernels for 13% -> 15%
where the time goes in v2:
time: 200 us; the launch traced here: 199 us
  waiting for transfers between devices  67.3 us (34%)
  Pallas kernels  37.6 us (19%)
  starting transfers between devices  36 us (18%)
  blocking collectives  27.7 us (14%)
  between operations  14.1 us (7%)
  local copies, waits for them, and re-layouts  11.3 us (6%)
  other arithmetic  5.32 us (3%)
    ppermute x26, waiting for transfers between devices, swap(): return lax.ppermute(x, axis, [(b, b ^ i) for b in range(count)])  57.2 us
    pallas_call x8, Pallas kernels, call(): pl.pallas_call(kernel, name=name, out_shape=[jax.ShapeDtypeStruct(shape,...  37.6 us
    ppermute x26, starting transfers between devices, swap(): return lax.ppermute(x, axis, [(b, b ^ i) for b in range(count)])  30.8 us
    all_to_all x1, blocking collectives, heads_body(): lax.all_to_all(grad_heads, 'ctx', 0, 0, tiled=True).reshape(tall)  27.7 us
    unnamed x25, local copies, waits for them, and re-layouts  10.7 us
    all_to_all x1, waiting for transfers between devices, heads_body(): lax.all_to_all(out_full.reshape(n, rows, HEAD_DIM), 'ctx', 0, 0, tiled=True)  10 us
    all_to_all x1, starting transfers between devices, heads_body(): lax.all_to_all(out_full.reshape(n, rows, HEAD_DIM), 'ctx', 0, 0, tiled=True)  5.19 us
  transfers between devices with their start and end apart: 28, of which 14 were waited for; matrix products, arithmetic and copies ran while one was open for 3% of the time, Pallas kernels for 15%

profile of v2, /device:TPU:9, one launch (start us, length us, event | category | flops | bytes accessed | tf_op | source)
XLA Modules:
  0.0 199.3 jit_solution(17807078497680777602)
XLA Ops:
  16.2 2.5 %collective-permute-start.8 = (bf16[3,256,128]{2,1,0:T(8,128)(2,1)S(1)}, bf16[3,256,128]{2,1,0:T(8,128)(2,1)S(1)}, u32[]{:S(2)}, u32[]{:S(2)}) collective-permute-start(bf16[3,256,128]{2,1,0:T(8,128)(2,1)S(1)} %get-tuple-element.50), channel_id=1, source_target_pairs={{0,12},{4,8},{8,4},{12,0},{16,28},{20,24},{24,20},{28,16},{1,13},{... | collective-permute-start | bytes 589832 | tf_op jit(solution)/shard_map/ppermute | solution.py:223
  18.8 2.3 %collective-permute-start.9 = (bf16[3,256,128]{2,1,0:T(8,128)(2,1)S(1)}, bf16[3,256,128]{2,1,0:T(8,128)(2,1)S(1)}, u32[]{:S(2)}, u32[]{:S(2)}) collective-permute-start(bf16[3,256,128]{2,1,0:T(8,128)(2,1)S(1)} %get-tuple-element.51), channel_id=1, source_target_pairs={{0,16},{4,20},{8,24},{12,28},{16,0},{20,4},{24,8},{28,12},{1,17},{... | collective-permute-start | bytes 589832 | tf_op jit(solution)/shard_map/ppermute | solution.py:223
  21.1 2.6 %collective-permute-start.10 = (bf16[3,256,128]{2,1,0:T(8,128)(2,1)S(1)}, bf16[3,256,128]{2,1,0:T(8,128)(2,1)S(1)}, u32[]{:S(2)}, u32[]{:S(2)}) collective-permute-start(bf16[3,256,128]{2,1,0:T(8,128)(2,1)S(1)} %get-tuple-element.52), channel_id=1, source_target_pairs={{0,20},{4,16},{8,28},{12,24},{16,4},{20,0},{24,12},{28,8},{1,21},{... | collective-permute-start | bytes 589832 | tf_op jit(solution)/shard_map/ppermute | solution.py:223
  24.1 9.4 %lookup.1 = (bf16[8,64,1024]{2,1,0:T(8,128)(2,1)S(1)}, bf16[8,64,1024]{2,1,0:T(8,128)(2,1)}, bf16[8,64,1024]{2,1,0:T(8,128)(2,1)}, bf16[8,64,1024]{2,1,0:T(8,128)(2,1)}) custom-call(s32[2]{0:T(128)S(1)} %pad_add_fusion.ids, bf16[8,512,1024]{2,1,0:T(8,128)(2,1)} %table_ref.1, s32[64,8]{1,0:T(8,128)S(1)} %copy.18.refs_0_, ...), custom_call_target="tpu_custom_call" | custom-call | flops 2147483648 | bytes 12591104 | tf_op jit(solution)/shard_map/lookup/pallas_call | solution.py:35
  33.4 1.6 collective-permute-start.5
  35.0 6.9 %collective-permute-done.9.refs_4_ = bf16[3,256,128]{2,1,0:T(8,128)(2,1)S(1)} collective-permute-done((bf16[3,256,128]{2,1,0:T(8,128)(2,1)S(1)}, bf16[3,256,128]{2,1,0:T(8,128)(2,1)S(1)}, u32[]{:S(2)}, u32[]{:S(2)}) %collective-permute-start.9) | collective-permute-done | bytes 196640 | tf_op jit(solution)/shard_map/ppermute | solution.py:223
  42.9 3.3 %collective-permute-done.10.refs_5_ = bf16[3,256,128]{2,1,0:T(8,128)(2,1)S(1)} collective-permute-done((bf16[3,256,128]{2,1,0:T(8,128)(2,1)S(1)}, bf16[3,256,128]{2,1,0:T(8,128)(2,1)S(1)}, u32[]{:S(2)}, u32[]{:S(2)}) %collective-permute-start.10) | collective-permute-done | bytes 196640 | tf_op jit(solution)/shard_map/ppermute | solution.py:223
  46.2 2.0 collective-permute-start.3
  48.2 2.6 %collective-permute-done.11.refs_6_ = bf16[3,256,128]{2,1,0:T(8,128)(2,1)S(1)} collective-permute-done((bf16[3,256,128]{2,1,0:T(8,128)(2,1)S(1)}, bf16[3,256,128]{2,1,0:T(8,128)(2,1)S(1)}, u32[]{:S(2)}, u32[]{:S(2)}) %collective-permute-start.11) | collective-permute-done | bytes 196640 | tf_op jit(solution)/shard_map/ppermute | solution.py:223
  50.8 4.4 %collective-permute-done.12.refs_7_ = bf16[3,256,128]{2,1,0:T(8,128)(2,1)S(1)} collective-permute-done((bf16[3,256,128]{2,1,0:T(8,128)(2,1)S(1)}, bf16[3,256,128]{2,1,0:T(8,128)(2,1)S(1)}, u32[]{:S(2)}, u32[]{:S(2)}) %collective-permute-start.12) | collective-permute-done | bytes 196640 | tf_op jit(solution)/shard_map/ppermute | solution.py:223
  55.2 6.5 %attend.1 = (bf16[2048,128]{1,0:T(8,128)(2,1)}, f32[1,2048]{1,0:T(1,128)S(1)}, bf16[2048,128]{1,0:T(8,128)(2,1)S(1)}, bf16[2048,128]{1,0:T(8,128)(2,1)S(1)}, bf16[2048,128]{1,0:T(8,128)(2,1)S(1)}) custom-call(s32[2]{0:T(128)S(1)} %pad_add_fusion.ids, s32[1,2048]{1,0:T(1,128)S(1)} %bitcast.14, bf16[3,256,128]{2,1,0:T(8,128)(2,1)S(1)} %get-tuple-element.47.refs_0_, ...), custom_call_target="tpu_custom_call" | custom-call | flops 1342177280 | bytes 3682304 | tf_op jit(solution)/shard_map/attend/pallas_call | solution.py:35
  64.1 5.2 %all-to-all-start = ((bf16[8,256,128]{2,1,0:T(8,128)(2,1)}), bf16[8,256,128]{2,1,0:T(8,128)(2,1)S(1)}, u32[]{:S(2)}, u32[]{:S(2)}) async-start(bf16[8,256,128]{2,1,0:T(8,128)(2,1)} %bitcast.5), calls=%async_computation | async-start | bytes 1048576 | tf_op jit(solution)/shard_map/all_to_all | solution.py:281
  69.3 1.8 copy.22
  71.1 10.0 %all-to-all-done.heads_ref = bf16[8,256,128]{2,1,0:T(8,128)(2,1)S(1)} async-done(((bf16[8,256,128]{2,1,0:T(8,128)(2,1)}), bf16[8,256,128]{2,1,0:T(8,128)(2,1)S(1)}, u32[]{:S(2)}, u32[]{:S(2)}) %all-to-all-start) | async-done | bytes 524320 | tf_op jit(solution)/shard_map/all_to_all | solution.py:281
  81.1 2.9 %project.1 = (bf16[256,1024]{1,0:T(8,128)(2,1)S(1)}, bf16[64,1024]{1,0:T(8,128)(2,1)S(1)}, bf16[64,1024]{1,0:T(8,128)(2,1)S(1)}, bf16[64,1024]{1,0:T(8,128)(2,1)S(1)}, bf16[64,1024]{1,0:T(8,128)(2,1)S(1)}) custom-call(s32[2]{0:T(128)S(1)} %pad_add_fusion.ids, bf16[4096,1024]{1,0:T(8,128)(2,1)} %w_ref.3, bf16[8,256,128]{2,1,0:T(8,128)(2,1)S(1)} %all-to-all-done.heads_ref), custom_call_target="tpu_custom_call" | custom-call | flops 536870912 | bytes 3670016 | tf_op jit(solution)/shard_map/project/pallas_call | solution.py:35
  86.8 2.8 %add_convert_fusion.embed_ref = bf16[8,64,1024]{2,1,0:T(8,128)(2,1)S(1)} fusion(bf16[8,64,1024]{2,1,0:T(8,128)(2,1)} %collective-permute-done.5, bf16[8,64,1024]{2,1,0:T(8,128)(2,1)} %collective-permute-done.4, bf16[8,64,1024]{2,1,0:T(8,128)(2,1)} %collective-permute-done.3, bf16[8,64,1024]{2,1,0:T(8,128)(2,1)S(1)} %get-tuple-element.43), kind=kLoop, calls=%fused_computation | loop fusion | flops 4194304 | bytes 5242880 | tf_op jit(solution)/shard_map/convert_element_type | solution.py:269
  89.6 2.5 %collective-permute-done.15.refs_3_ = bf16[64,1024]{1,0:T(8,128)(2,1)S(1)} collective-permute-done((bf16[64,1024]{1,0:T(8,128)(2,1)S(1)}, bf16[64,1024]{1,0:T(8,128)(2,1)S(1)}, u32[]{:S(2)}, u32[]{:S(2)}) %collective-permute-start.15) | collective-permute-done | bytes 131104 | tf_op jit(solution)/shard_map/ppermute | solution.py:223
  92.1 1.9 depth.1
  98.2 3.9 %collective-permute-done.17.refs_2_ = bf16[80,1024]{1,0:T(8,128)(2,1)S(1)} collective-permute-done((bf16[80,1024]{1,0:T(8,128)(2,1)S(1)}, bf16[80,1024]{1,0:T(8,128)(2,1)S(1)}, u32[]{:S(2)}, u32[]{:S(2)}) %collective-permute-start.17) | collective-permute-done | bytes 163872 | tf_op jit(solution)/shard_map/ppermute | solution.py:223
  102.2 4.8 %grad_attn.1 = (bf16[8,256,128]{2,1,0:T(8,128)(2,1)S(1)}, bf16[8,1040,128]{2,1,0:T(8,128)(2,1)}) custom-call(s32[2]{0:T(128)S(1)} %pad_add_fusion.ids, bf16[4096,1024]{1,0:T(8,128)(2,1)} %w_ref.3, bf16[256,1024]{1,0:T(8,128)(2,1)S(1)} %get-tuple-element.65.attn_ref, bf16[80,1024]{1,0:T(8,128)(2,1)S(1)} %get-tuple-element.66.refs_0_, ...), custom_call_target="tpu_custom_call" | custom-call | flops 1073741824 | bytes 5931008 | tf_op jit(solution)/shard_map/grad_attn/pallas_call | solution.py:35
  107.0 27.7 %all_to_all.10 = bf16[8,256,128]{2,1,0:T(8,128)(2,1)} all-to-all(bf16[8,256,128]{2,1,0:T(8,128)(2,1)S(1)} %get-tuple-element.67), channel_id=1, replica_groups=mesh['ctx'=8,'tp'=4] {'ctx'}, dimensions={0} | all-to-all | bytes 1048576 | tf_op jit(solution)/shard_map/all_to_all | solution.py:319
  135.8 8.3 %attend_grad.1 = (bf16[3,256,128]{2,1,0:T(8,128)(2,1)S(1)}, bf16[3,256,128]{2,1,0:T(8,128)(2,1)S(1)}, bf16[3,256,128]{2,1,0:T(8,128)(2,1)S(1)}, bf16[3,256,128]{...) custom-call(s32[2]{0:T(128)S(1)} %pad_add_fusion.ids, ...), custom_call_target="tpu_custom_call" | custom-call | flops 3355443200 | bytes 4210688 | tf_op jit(solution)/shard_map/attend_grad/pallas_call | solution.py:35
  144.1 1.7 collective-permute-start.19
  145.8 3.2 %collective-permute-start.20 = (bf16[3,256,128]{2,1,0:T(8,128)(2,1)S(1)}, bf16[3,256,128]{2,1,0:T(8,128)(2,1)S(1)}, u32[]{:S(2)}, u32[]{:S(2)}) collective-permute-start(bf16[3,256,128]{2,1,0:T(8,128)(2,1)S(1)} %get-tuple-element.70), channel_id=1, source_target_pairs={{0,8},{4,12},{8,0},{12,4},{16,24},{20,28},{24,16},{28,20},{1,9},{5... | collective-permute-start | bytes 589832 | tf_op jit(solution)/shard_map/ppermute | solution.py:223
  150.1 1.9 collective-permute-start.23
  152.0 8.9 %collective-permute-done.20.refs_2_ = bf16[3,256,128]{2,1,0:T(8,128)(2,1)S(1)} collective-permute-done((bf16[3,256,128]{2,1,0:T(8,128)(2,1)S(1)}, bf16[3,256,128]{2,1,0:T(8,128)(2,1)S(1)}, u32[]{:S(2)}, u32[]{:S(2)}) %collective-permute-start.20) | collective-permute-done | bytes 196640 | tf_op jit(solution)/shard_map/ppermute | solution.py:223
  160.8 1.7 collective-permute-start.25
  165.2 3.1 %collective-permute-done.23.refs_5_ = bf16[3,256,128]{2,1,0:T(8,128)(2,1)S(1)} collective-permute-done((bf16[3,256,128]{2,1,0:T(8,128)(2,1)S(1)}, bf16[3,256,128]{2,1,0:T(8,128)(2,1)S(1)}, u32[]{:S(2)}, u32[]{:S(2)}) %collective-permute-start.23) | collective-permute-done | bytes 196640 | tf_op jit(solution)/shard_map/ppermute | solution.py:223
  168.2 14.4 %collective-permute-done.24.refs_6_ = bf16[3,256,128]{2,1,0:T(8,128)(2,1)S(1)} collective-permute-done((bf16[3,256,128]{2,1,0:T(8,128)(2,1)S(1)}, bf16[3,256,128]{2,1,0:T(8,128)(2,1)S(1)}, u32[]{:S(2)}, u32[]{:S(2)}) %collective-permute-start.24) | collective-permute-done | bytes 196640 | tf_op jit(solution)/shard_map/ppermute | solution.py:223
  182.6 4.2 %collective-permute-done.25.refs_7_ = bf16[3,256,128]{2,1,0:T(8,128)(2,1)S(1)} collective-permute-done((bf16[3,256,128]{2,1,0:T(8,128)(2,1)S(1)}, bf16[3,256,128]{2,1,0:T(8,128)(2,1)S(1)}, u32[]{:S(2)}, u32[]{:S(2)}) %collective-permute-start.25) | collective-permute-done | bytes 196640 | tf_op jit(solution)/shard_map/ppermute | solution.py:223
  186.8 2.6 %assemble.1 = (f32[256,1024]{1,0:T(8,128)}, f32[256,1024]{1,0:T(8,128)}, f32[256,1024]{1,0:T(8,128)}) custom-call(s32[2]{0:T(128)S(1)} %pad_add_fusion.ids, bf16[3,256,128]{2,1,0:T(8,128)(2,1)S(1)} %get-tuple-element.68.refs_0_, bf16[3,256,128]{2,1,0:T(8,128)(2,1)S(1)} %collective-permute-done.19.refs_1_, ...), custom_call_target="tpu_custom_call" | custom-call | bytes 3145728 | tf_op jit(solution)/shard_map/assemble/pallas_call | solution.py:35
  190.7 1.8 slice_convert_fusion
  (64 shorter events, 25.7 us)
Async XLA Ops:
  11.6 12.1 %collective-permute-start.6 = (bf16[3,256,128]{2,1,0:T(8,128)(2,1)S(1)}, bf16[3,256,128]{2,1,0:T(8,128)(2,1)S(1)}, u32[]{:S(2)}, u32[]{:S(2)}) collective-permute-start(bf16[3,256,128]{2,1,0:T(8,128)(2,1)S(1)} %get-tuple-element.48), channel_id=1, source_target_pairs={{0,4},{4,0},{8,12},{12,8},{16,20},{20,16},{24,28},{28,24},{1,5},{5... | collective-permute-start | bytes 589832 | tf_op jit(solution)/shard_map/ppermute | solution.py:223
  12.4 11.7 %collective-permute-start.7 = (bf16[3,256,128]{2,1,0:T(8,128)(2,1)S(1)}, bf16[3,256,128]{2,1,0:T(8,128)(2,1)S(1)}, u32[]{:S(2)}, u32[]{:S(2)}) collective-permute-start(bf16[3,256,128]{2,1,0:T(8,128)(2,1)S(1)} %get-tuple-element.49), channel_id=1, source_target_pairs={{0,8},{4,12},{8,0},{12,4},{16,24},{20,28},{24,16},{28,20},{1,9},{5... | collective-permute-start | bytes 589832 | tf_op jit(solution)/shard_map/ppermute | solution.py:223
  13.1 3.1 %collective-permute-start = (s32[64,8]{1,0:T(8,128)S(1)}, s32[64,8]{1,0:T(8,128)S(1)}, u32[]{:S(2)}, u32[]{:S(2)}) collective-permute-start(s32[64,8]{1,0:T(8,128)S(1)} %copy.18.refs_0_), channel_id=1, source_target_pairs={{0,1},{1,0},{2,3},{3,2},{4,5},{5,4},{6,7},{7,6},{8,9},{9,8},{10,11... | collective-permute-start | bytes 6152 | tf_op jit(solution)/shard_map/ppermute | solution.py:223
  14.6 4.2 %collective-permute-start.1 = (s32[64,8]{1,0:T(8,128)S(1)}, s32[64,8]{1,0:T(8,128)S(1)}, u32[]{:S(2)}, u32[]{:S(2)}) collective-permute-start(s32[64,8]{1,0:T(8,128)S(1)} %copy.18.refs_0_), channel_id=1, source_target_pairs={{0,2},{1,3},{2,0},{3,1},{4,6},{5,7},{6,4},{7,5},{8,10},{9,11},{10,... | collective-permute-start | bytes 6152 | tf_op jit(solution)/shard_map/ppermute | solution.py:223
  15.8 5.3 %collective-permute-start.2 = (s32[64,8]{1,0:T(8,128)S(1)}, s32[64,8]{1,0:T(8,128)S(1)}, u32[]{:S(2)}, u32[]{:S(2)}) collective-permute-start(s32[64,8]{1,0:T(8,128)S(1)} %copy.18.refs_0_), channel_id=1, source_target_pairs={{0,3},{1,2},{2,1},{3,0},{4,7},{5,6},{6,5},{7,4},{8,11},{9,10},{10,... | collective-permute-start | bytes 6152 | tf_op jit(solution)/shard_map/ppermute | solution.py:223
  16.2 17.2 %collective-permute-start.8 = (bf16[3,256,128]{2,1,0:T(8,128)(2,1)S(1)}, bf16[3,256,128]{2,1,0:T(8,128)(2,1)S(1)}, u32[]{:S(2)}, u32[]{:S(2)}) collective-permute-start(bf16[3,256,128]{2,1,0:T(8,128)(2,1)S(1)} %get-tuple-element.50), channel_id=1, source_target_pairs={{0,12},{4,8},{8,4},{12,0},{16,28},{20,24},{24,20},{28,16},{1,13},{... | collective-permute-start | bytes 589832 | tf_op jit(solution)/shard_map/ppermute | solution.py:223
  18.8 23.1 %collective-permute-start.9 = (bf16[3,256,128]{2,1,0:T(8,128)(2,1)S(1)}, bf16[3,256,128]{2,1,0:T(8,128)(2,1)S(1)}, u32[]{:S(2)}, u32[]{:S(2)}) collective-permute-start(bf16[3,256,128]{2,1,0:T(8,128)(2,1)S(1)} %get-tuple-element.51), channel_id=1, source_target_pairs={{0,16},{4,20},{8,24},{12,28},{16,0},{20,4},{24,8},{28,12},{1,17},{... | collective-permute-start | bytes 589832 | tf_op jit(solution)/shard_map/ppermute | solution.py:223
  21.1 25.0 %collective-permute-start.10 = (bf16[3,256,128]{2,1,0:T(8,128)(2,1)S(1)}, bf16[3,256,128]{2,1,0:T(8,128)(2,1)S(1)}, u32[]{:S(2)}, u32[]{:S(2)}) collective-permute-start(bf16[3,256,128]{2,1,0:T(8,128)(2,1)S(1)} %get-tuple-element.52), channel_id=1, source_target_pairs={{0,20},{4,16},{8,28},{12,24},{16,4},{20,0},{24,12},{28,8},{1,21},{... | collective-permute-start | bytes 589832 | tf_op jit(solution)/shard_map/ppermute | solution.py:223
  23.7 27.0 %collective-permute-start.11 = (bf16[3,256,128]{2,1,0:T(8,128)(2,1)S(1)}, bf16[3,256,128]{2,1,0:T(8,128)(2,1)S(1)}, u32[]{:S(2)}, u32[]{:S(2)}) collective-permute-start(bf16[3,256,128]{2,1,0:T(8,128)(2,1)S(1)} %get-tuple-element.53), channel_id=1, source_target_pairs={{0,24},{4,28},{8,16},{12,20},{16,8},{20,12},{24,0},{28,4},{1,25},{... | collective-permute-start | bytes 589832 | tf_op jit(solution)/shard_map/ppermute | solution.py:223
  24.1 31.1 %copy-start.4 = (s32[2048]{0:T(1024)S(1)}, s32[2048]{0:T(1024)}, u32[]{:S(2)}) copy-start(s32[2048]{0:T(1024)} %param.12) | copy-start | bytes 24580
  24.1 31.1 %collective-permute-start.12 = (bf16[3,256,128]{2,1,0:T(8,128)(2,1)S(1)}, bf16[3,256,128]{2,1,0:T(8,128)(2,1)S(1)}, u32[]{:S(2)}, u32[]{:S(2)}) collective-permute-start(bf16[3,256,128]{2,1,0:T(8,128)(2,1)S(1)} %get-tuple-element.54), channel_id=1, source_target_pairs={{0,28},{4,24},{8,20},{12,16},{16,12},{20,8},{24,4},{28,0},{1,29},{... | collective-permute-start | bytes 589832 | tf_op jit(solution)/shard_map/ppermute | solution.py:223
  33.4 53.2 %collective-permute-start.5 = (bf16[8,64,1024]{2,1,0:T(8,128)(2,1)}, bf16[8,64,1024]{2,1,0:T(8,128)(2,1)}, u32[]{:S(2)}, u32[]{:S(2)}) collective-permute-start(bf16[8,64,1024]{2,1,0:T(8,128)(2,1)} %get-tuple-element.46), channel_id=1, source_target_pairs={{0,3},{1,2},{2,1},{3,0},{4,7},{5,6},{6,5},{7,4},{8,11},{9,10},{10,... | collective-permute-start | bytes 3145736 | tf_op jit(solution)/shard_map/ppermute | solution.py:223
  42.0 44.8 %collective-permute-start.4 = (bf16[8,64,1024]{2,1,0:T(8,128)(2,1)}, bf16[8,64,1024]{2,1,0:T(8,128)(2,1)}, u32[]{:S(2)}, u32[]{:S(2)}) collective-permute-start(bf16[8,64,1024]{2,1,0:T(8,128)(2,1)} %get-tuple-element.45), channel_id=1, source_target_pairs={{0,2},{1,3},{2,0},{3,1},{4,6},{5,7},{6,4},{7,5},{8,10},{9,11},{10,... | collective-permute-start | bytes 3145736 | tf_op jit(solution)/shard_map/ppermute | solution.py:223
  46.2 40.6 %collective-permute-start.3 = (bf16[8,64,1024]{2,1,0:T(8,128)(2,1)}, bf16[8,64,1024]{2,1,0:T(8,128)(2,1)}, u32[]{:S(2)}, u32[]{:S(2)}) collective-permute-start(bf16[8,64,1024]{2,1,0:T(8,128)(2,1)} %get-tuple-element.44), channel_id=1, source_target_pairs={{0,1},{1,0},{2,3},{3,2},{4,5},{5,4},{6,7},{7,6},{8,9},{9,8},{10,11... | collective-permute-start | bytes 3145736 | tf_op jit(solution)/shard_map/ppermute | solution.py:223
  64.1 17.0 %all-to-all-start = ((bf16[8,256,128]{2,1,0:T(8,128)(2,1)}), bf16[8,256,128]{2,1,0:T(8,128)(2,1)S(1)}, u32[]{:S(2)}, u32[]{:S(2)}) async-start(bf16[8,256,128]{2,1,0:T(8,128)(2,1)} %bitcast.5), calls=%async_computation | async-start | bytes 1048576 | tf_op jit(solution)/shard_map/all_to_all | solution.py:281
  69.3 120.1 %reduce-scatter.2.cloned.1.call-start = ((), (), s32[]{:S(2)}) async-start(), calls=%async_computation.3 | async-start | bytes 2396160 | tf_op jit(solution)/shard_map/reduce_scatter | solution.py:316
  84.0 5.5 %collective-permute-start.13 = (bf16[64,1024]{1,0:T(8,128)(2,1)S(1)}, bf16[64,1024]{1,0:T(8,128)(2,1)S(1)}, u32[]{:S(2)}, u32[]{:S(2)}) collective-permute-start(bf16[64,1024]{1,0:T(8,128)(2,1)S(1)} %get-tuple-element.57), channel_id=1, source_target_pairs={{0,1},{1,0},{2,3},{3,2},{4,5},{5,4},{6,7},{7,6},{8,9},{9,8},{10,11... | collective-permute-start | bytes 393224 | tf_op jit(solution)/shard_map/ppermute | solution.py:223
  85.3 4.2 %collective-permute-start.14 = (bf16[64,1024]{1,0:T(8,128)(2,1)S(1)}, bf16[64,1024]{1,0:T(8,128)(2,1)S(1)}, u32[]{:S(2)}, u32[]{:S(2)}) collective-permute-start(bf16[64,1024]{1,0:T(8,128)(2,1)S(1)} %get-tuple-element.58), channel_id=1, source_target_pairs={{0,2},{1,3},{2,0},{3,1},{4,6},{5,7},{6,4},{7,5},{8,10},{9,11},{10,... | collective-permute-start | bytes 393224 | tf_op jit(solution)/shard_map/ppermute | solution.py:223
  86.6 5.5 %collective-permute-start.15 = (bf16[64,1024]{1,0:T(8,128)(2,1)S(1)}, bf16[64,1024]{1,0:T(8,128)(2,1)S(1)}, u32[]{:S(2)}, u32[]{:S(2)}) collective-permute-start(bf16[64,1024]{1,0:T(8,128)(2,1)S(1)} %get-tuple-element.59), channel_id=1, source_target_pairs={{0,3},{1,2},{2,1},{3,0},{4,7},{5,6},{6,5},{7,4},{8,11},{9,10},{10,... | collective-permute-start | bytes 393224 | tf_op jit(solution)/shard_map/ppermute | solution.py:223
  86.8 5.3 %copy-start.3 = (f32[1024]{0:T(1024)S(1)}, f32[1024]{0:T(1024)}, u32[]{:S(2)}) copy-start(f32[1024]{0:T(1024)} %param.16) | copy-start | bytes 12292
  94.0 4.2 %collective-permute-start.16 = (bf16[80,1024]{1,0:T(8,128)(2,1)S(1)}, bf16[80,1024]{1,0:T(8,128)(2,1)S(1)}, u32[]{:S(2)}, u32[]{:S(2)}) collective-permute-start(bf16[80,1024]{1,0:T(8,128)(2,1)S(1)} %get-tuple-element.66.refs_0_), channel_id=1, source_target_pairs={{0,1},{1,0},{2,3},{3,2},{4,5},{5,4},{6,7},{7,6},{8,9},{9,8},{10,11... | collective-permute-start | bytes 491528 | tf_op jit(solution)/shard_map/ppermute | solution.py:223
  95.5 6.7 %collective-permute-start.17 = (bf16[80,1024]{1,0:T(8,128)(2,1)S(1)}, bf16[80,1024]{1,0:T(8,128)(2,1)S(1)}, u32[]{:S(2)}, u32[]{:S(2)}) collective-permute-start(bf16[80,1024]{1,0:T(8,128)(2,1)S(1)} %get-tuple-element.66.refs_0_), channel_id=1, source_target_pairs={{0,2},{1,3},{2,0},{3,1},{4,6},{5,7},{6,4},{7,5},{8,10},{9,11},{10,... | collective-permute-start | bytes 491528 | tf_op jit(solution)/shard_map/ppermute | solution.py:223
  95.7 6.5 %collective-permute-start.18 = (bf16[80,1024]{1,0:T(8,128)(2,1)S(1)}, bf16[80,1024]{1,0:T(8,128)(2,1)S(1)}, u32[]{:S(2)}, u32[]{:S(2)}) collective-permute-start(bf16[80,1024]{1,0:T(8,128)(2,1)S(1)} %get-tuple-element.66.refs_0_), channel_id=1, source_target_pairs={{0,3},{1,2},{2,1},{3,0},{4,7},{5,6},{6,5},{7,4},{8,11},{9,10},{10,... | collective-permute-start | bytes 491528 | tf_op jit(solution)/shard_map/ppermute | solution.py:223
  106.9 27.8 %copy-start.6 = (bf16[2048,128]{1,0:T(8,128)(2,1)S(1)}, bf16[2048,128]{1,0:T(8,128)(2,1)}, u32[]{:S(2)}) copy-start(bf16[2048,128]{1,0:T(8,128)(2,1)} %copy-done.5) | copy-start | bytes 1572868
  106.9 27.8 %copy-start.8 = (bf16[2048,128]{1,0:T(8,128)(2,1)S(1)}, bf16[2048,128]{1,0:T(8,128)(2,1)}, u32[]{:S(2)}) copy-start(bf16[2048,128]{1,0:T(8,128)(2,1)} %copy-done.7) | copy-start | bytes 1572868
  144.1 7.9 %collective-permute-start.19 = (bf16[3,256,128]{2,1,0:T(8,128)(2,1)S(1)}, bf16[3,256,128]{2,1,0:T(8,128)(2,1)S(1)}, u32[]{:S(2)}, u32[]{:S(2)}) collective-permute-start(bf16[3,256,128]{2,1,0:T(8,128)(2,1)S(1)} %get-tuple-element.69), channel_id=1, source_target_pairs={{0,4},{4,0},{8,12},{12,8},{16,20},{20,16},{24,28},{28,24},{1,5},{5... | collective-permute-start | bytes 589832 | tf_op jit(solution)/shard_map/ppermute | solution.py:223
  145.8 15.0 %collective-permute-start.20 = (bf16[3,256,128]{2,1,0:T(8,128)(2,1)S(1)}, bf16[3,256,128]{2,1,0:T(8,128)(2,1)S(1)}, u32[]{:S(2)}, u32[]{:S(2)}) collective-permute-start(bf16[3,256,128]{2,1,0:T(8,128)(2,1)S(1)} %get-tuple-element.70), channel_id=1, source_target_pairs={{0,8},{4,12},{8,0},{12,4},{16,24},{20,28},{24,16},{28,20},{1,9},{5... | collective-permute-start | bytes 589832 | tf_op jit(solution)/shard_map/ppermute | solution.py:223
  149.0 16.1 %collective-permute-start.21 = (bf16[3,256,128]{2,1,0:T(8,128)(2,1)}, bf16[3,256,128]{2,1,0:T(8,128)(2,1)S(1)}, u32[]{:S(2)}, u32[]{:S(2)}) collective-permute-start(bf16[3,256,128]{2,1,0:T(8,128)(2,1)} %get-tuple-element.71), channel_id=1, source_target_pairs={{0,12},{4,8},{8,4},{12,0},{16,28},{20,24},{24,20},{28,16},{1,13},{... | collective-permute-start | bytes 589832 | tf_op jit(solution)/shard_map/ppermute | solution.py:223
  149.0 16.1 %collective-permute-start.22 = (bf16[3,256,128]{2,1,0:T(8,128)(2,1)S(1)}, bf16[3,256,128]{2,1,0:T(8,128)(2,1)S(1)}, u32[]{:S(2)}, u32[]{:S(2)}) collective-permute-start(bf16[3,256,128]{2,1,0:T(8,128)(2,1)S(1)} %get-tuple-element.72), channel_id=1, source_target_pairs={{0,16},{4,20},{8,24},{12,28},{16,0},{20,4},{24,8},{28,12},{1,17},{... | collective-permute-start | bytes 589832 | tf_op jit(solution)/shard_map/ppermute | solution.py:223
  150.1 18.1 %collective-permute-start.23 = (bf16[3,256,128]{2,1,0:T(8,128)(2,1)S(1)}, bf16[3,256,128]{2,1,0:T(8,128)(2,1)S(1)}, u32[]{:S(2)}, u32[]{:S(2)}) collective-permute-start(bf16[3,256,128]{2,1,0:T(8,128)(2,1)S(1)} %get-tuple-element.73), channel_id=1, source_target_pairs={{0,20},{4,16},{8,28},{12,24},{16,4},{20,0},{24,12},{28,8},{1,21},{... | collective-permute-start | bytes 589832 | tf_op jit(solution)/shard_map/ppermute | solution.py:223
  152.0 30.6 %collective-permute-start.24 = (bf16[3,256,128]{2,1,0:T(8,128)(2,1)S(1)}, bf16[3,256,128]{2,1,0:T(8,128)(2,1)S(1)}, u32[]{:S(2)}, u32[]{:S(2)}) collective-permute-start(bf16[3,256,128]{2,1,0:T(8,128)(2,1)S(1)} %get-tuple-element.74), channel_id=1, source_target_pairs={{0,24},{4,28},{8,16},{12,20},{16,8},{20,12},{24,0},{28,4},{1,25},{... | collective-permute-start | bytes 589832 | tf_op jit(solution)/shard_map/ppermute | solution.py:223
  160.8 26.0 %collective-permute-start.25 = (bf16[3,256,128]{2,1,0:T(8,128)(2,1)S(1)}, bf16[3,256,128]{2,1,0:T(8,128)(2,1)S(1)}, u32[]{:S(2)}, u32[]{:S(2)}) collective-permute-start(bf16[3,256,128]{2,1,0:T(8,128)(2,1)S(1)} %get-tuple-element.75), channel_id=1, source_target_pairs={{0,28},{4,24},{8,20},{12,16},{16,12},{20,8},{24,4},{28,0},{1,29},{... | collective-permute-start | bytes 589832 | tf_op jit(solution)/shard_map/ppermute | solution.py:223
  (7 other events, 6.5 us)
Sparse Core Ops, SparseCore 0:
  107.1 47.5 reduce-scatter.1

commit v3 on v2

--- a/solution.py
+++ b/solution.py
@@ -15,7 +15,8 @@
 EPSILON = 1e-06
 LOG2_E = 1.4426950408889634
 SEGMENT_VALUES = 4
-VMEM_BYTES = 50 << 20
+GAIN_SLOTS = 8
+MIB = 1 << 20
 F32 = jnp.float32
 BF16 = jnp.bfloat16
 
@@ -24,7 +25,7 @@
     return lax.dot_general(a, b, (((a_dim,), (b_dim,)), ((), ())), preferred_element_type=F32)
 
 
-def call(kernel, name, ids, inputs, out_shapes, scratch=(), in_specs=None, out_specs=None, grid=(1,), flops=0, extra=0, skip=0):
+def call(kernel, name, ids, inputs, out_shapes, scratch=(), in_specs=None, out_specs=None, grid=(1,), flops=0, vmem=16, costly=True):
     def whole(shape):
         return pl.BlockSpec(shape, lambda step, ids: (0,) * len(shape))
 
@@ -43,11 +44,11 @@
             out_specs=[out_specs.get(n, whole(shape)) for n, (shape, _) in enumerate(out_shapes)],
             scratch_shapes=list(scratch),
         ),
-        compiler_params=pltpu.CompilerParams(vmem_limit_bytes=VMEM_BYTES),
+        compiler_params=pltpu.CompilerParams(vmem_limit_bytes=vmem * MIB),
         cost_estimate=pl.CostEstimate(
             flops=flops,
             transcendentals=0,
-            bytes_accessed=extra + sum(x.size * x.dtype.itemsize for x in inputs[skip:]) + sum(math.prod(o[0]) * 2 for o in out_shapes),
+            bytes_accessed=0 if not costly else sum(x.size * x.dtype.itemsize for x in inputs) + sum(math.prod(o[0]) * 2 for o in out_shapes),
         ),
     )(ids, *inputs)
 
@@ -56,14 +57,12 @@
     return pl.multiple_of(index * width, width)
 
 
-def pack_kernel(n, width, ids, q_ref, k_ref, v_ref, *refs):
-    outs, sem = refs[:n], refs[n]
-    me = ids[0]
+def pack_kernel(n, ids, q_ref, k_ref, v_ref, out_ref, sem):
     copies = []
-    for i in range(n):
-        columns = pl.ds(offset(me ^ i, width), width)
-        for part, ref in enumerate((q_ref, k_ref, v_ref)):
-            copies.append(pltpu.make_async_copy(ref.at[:, columns], outs[i].at[part], sem.at[3 * i + part]))
+    for part, ref in enumerate((q_ref, k_ref, v_ref)):
+        for i in range(n):
+            columns = ref.at[:, i * HEAD_DIM : (i + 1) * HEAD_DIM]
+            copies.append(pltpu.make_async_copy(columns, out_ref.at[i, part], sem.at[part * n + i]))
             copies[-1].start()
     for copy in copies:
         copy.wait()
@@ -83,56 +82,64 @@
     return (key_pos >= starts[:, first : first + rows]) & (key_pos <= query_pos)
 
 
-def forward_kernel(n, rows, window, factor, ids, seg_ref, *refs):
-    pieces = refs[:n]
-    out_ref, norm_ref, q_s, k_s, v_s = refs[n:]
-    me = ids[0]
-    for i in range(n):
-        place = pl.ds(offset(me ^ i, rows), rows)
-        q_s[place, :] = pieces[i][0]
-        k_s[place, :] = pieces[i][1]
-        v_s[place, :] = pieces[i][2]
+def rows_of(pieces_ref, part, low, high):
+    return jnp.concatenate([pieces_ref[i, part] for i in range(low, high)], axis=0)
+
+
+def forward_kernel(n, rows, window, factor, ids, seg_ref, pieces_ref, out_ref, norm_ref):
     starts = segment_starts(seg_ref[...])
     for block in range(n):
         first, low = block * rows, max(0, block - window) * rows
         count = first + rows - low
-        scores = dot(k_s[low : low + count, :], q_s[first : first + rows, :], 1, 1) * factor
+        keys = rows_of(pieces_ref, 1, low // rows, block + 1)
+        values = rows_of(pieces_ref, 2, low // rows, block + 1)
+        scores = dot(keys, pieces_ref[block, 0], 1, 1) * factor
         scores = jnp.where(visible(starts, low, count, first, rows), scores, NEGATIVE)
         top = jnp.max(scores, axis=0, keepdims=True)
         mass = jnp.exp2(scores - top)
         total = jnp.sum(mass, axis=0, keepdims=True)
-        mixed = dot(v_s[low : low + count, :], mass.astype(BF16), 0, 0) / total
+        mixed = dot(values, mass.astype(BF16), 0, 0) / total
         out_ref[first : first + rows, :] = mixed.T.astype(BF16)
         norm_ref[:, first : first + rows] = top + jnp.log2(total)
 
 
-def backward_kernel(n, rows, window, factor, scale, ids, seg_ref, norm_ref, out_ref, q_s, k_s, v_s, g_s, *refs):
-    outs = refs[:n]
-    dq_s, dk_s, dv_s = refs[n:]
-    me = ids[0]
+def probs_kernel(n, rows, window, factor, ids, seg_ref, norm_ref, pieces_ref, probs_ref):
     starts = segment_starts(seg_ref[...])
+    place = 0
     for block in range(n):
         first, low = block * rows, max(0, block - window) * rows
         count = first + rows - low
-        keys, query, grad = k_s[low : low + count, :], q_s[first : first + rows, :], g_s[first : first + rows, :]
-        scores = dot(keys, query, 1, 1) * factor - norm_ref[:, first : first + rows]
+        keys = rows_of(pieces_ref, 1, low // rows, block + 1)
+        scores = dot(keys, pieces_ref[block, 0], 1, 1) * factor - norm_ref[:, first : first + rows]
         probs = jnp.exp2(jnp.where(visible(starts, low, count, first, rows), scores, NEGATIVE))
+        probs_ref[place : place + count, :] = probs.astype(BF16)
+        place += count
+
+
+def backward_kernel(n, rows, window, scale, ids, probs_ref, out_ref, pieces_ref, g_s, grads_ref, dk_s, dv_s):
+    place = 0
+    for block in range(n):
+        first, low = block * rows, max(0, block - window) * rows
+        count = first + rows - low
+        keys = rows_of(pieces_ref, 1, low // rows, block + 1)
+        values = rows_of(pieces_ref, 2, low // rows, block + 1)
+        query, grad = pieces_ref[block, 0], g_s[first : first + rows, :]
+        probs = probs_ref[place : place + count, :]
+        place += count
         product = grad.astype(F32) * out_ref[first : first + rows, :].astype(F32)
         delta = jnp.sum(product.T, axis=0, keepdims=True)
-        score_grad = (probs * (dot(v_s[low : low + count, :], grad, 1, 1) - delta)).astype(BF16)
-        dq_s[first : first + rows, :] = (dot(keys, score_grad, 0, 0).T * scale).astype(BF16)
+        score_grad = (probs.astype(F32) * (dot(values, grad, 1, 1) - delta)).astype(BF16)
+        grads_ref[block, 0] = (dot(keys, score_grad, 0, 0).T * scale).astype(BF16)
         key_grad = dot(score_grad, query, 1, 0)
-        value_grad = dot(probs.astype(BF16), grad, 1, 0)
+        value_grad = dot(probs, grad, 1, 0)
         if count > rows:
             dk_s[low:first, :] += key_grad[: count - rows]
             dv_s[low:first, :] += value_grad[: count - rows]
         dk_s[first : first + rows, :] = key_grad[count - rows :]
         dv_s[first : first + rows, :] = value_grad[count - rows :]
     for i in range(n):
-        place = pl.ds(offset(me ^ i, rows), rows)
-        outs[i][0] = dq_s[place, :]
-        outs[i][1] = (dk_s[place, :] * scale).astype(BF16)
-        outs[i][2] = dv_s[place, :].astype(BF16)
+        grads_ref[i, 1] = (dk_s[i * rows : (i + 1) * rows, :] * scale).astype(BF16)
+        grads_ref[i, 2] = dv_s[i * rows : (i + 1) * rows, :].astype(BF16)
 
 
 def project_kernel(n, t, ids, w_ref, heads_ref, *refs):
@@ -146,8 +153,9 @@
         outs[i][...] = total[pl.ds(offset(shard ^ i, rows), rows), :]
 
 
-def lookup_kernel(t, ids, table_ref, *refs):
-    codes, outs = refs[:t], refs[t:]
+def lookup_kernel(t, ids, table_ref, w_ref, *refs):
+    codes, outs, w_out_ref = refs[:t], refs[t : 2 * t], refs[2 * t]
+    w_out_ref[...] = w_ref[...]
     book = pl.program_id(0)
     shard_rows, rows = table_ref.shape[1], codes[0].shape[0]
     picks = []
@@ -190,10 +198,12 @@
     return jnp.where(place == 2 * slot, high, jnp.where(place == 2 * slot + 1, row - high, 0.0)).astype(BF16)
 
 
-def grad_attn_kernel(n, t, ids, w_ref, attn_ref, *refs):
-    parts, out_ref, proj_ref, sum_s = refs[:t], refs[t], refs[t + 1], refs[t + 2]
+def grad_attn_kernel(n, t, ids, w_ref, *refs):
+    parts, out_ref, keep_ref, send_ref, sum_s = refs[:t], refs[t], refs[t + 1], refs[t + 2], refs[t + 3]
     me, shard = ids[0], ids[1]
     rows = sum_s.shape[0] // t
+    total = sum_s.shape[0]
+    columns = keep_ref.shape[2]
     gain = jnp.zeros((1, sum_s.shape[1]), F32)
     for i in range(t):
         sum_s[pl.ds(offset(shard ^ i, rows), rows), :] = parts[i][:rows, :]
@@ -201,22 +211,49 @@
     grad = dot(sum_s[...], w_ref[...], 1, 1).astype(BF16)
     for i in range(n):
         out_ref[i] = grad[:, i * HEAD_DIM : (i + 1) * HEAD_DIM]
-    term = dot(attn_ref[...], sum_s[...], 0, 0).astype(BF16)
-    tail = two_parts(gain, me, 2 * n)
-    width, columns = term.shape[0], proj_ref.shape[2]
+    core = me & 1
+    gains = two_parts(gain, core, 2 * GAIN_SLOTS)
+    for i in range(n // 2):
+        even = slice(2 * i * columns, (2 * i + 1) * columns)
+        odd = slice((2 * i + 1) * columns, (2 * i + 2) * columns)
+        for ref, flip in ((keep_ref, core), (send_ref, 1 - core)):
+            ref[i, :total, :] = jnp.where(flip == 0, sum_s[:, even], sum_s[:, odd])
+            ref[i, total:, :] = jnp.where(flip == 0, gains[:, even], gains[:, odd])
+
+
+def halving_order(n):
+    order = [0]
+    step = n // 2
+    while step:
+        order = order + [k + step for k in order]
+        step //= 2
+    return order
+
+
+def grad_proj_kernel(n, ids, attn_ref, other_attn_ref, sum_ref, other_sum_ref, keep_ref, send_ref):
+    chip = lax.shift_right_logical(ids[0], 1)
+    rows, width = attn_ref.shape
+    half = n // 4
+    for i, k in enumerate(halving_order(n // 2)):
+        term = dot(attn_ref[...], sum_ref[chip ^ k, :rows, :], 0, 0)
+        term = term + dot(other_attn_ref[...], other_sum_ref[chip ^ k, :rows, :], 0, 0)
+        tails = sum_ref[chip ^ k, rows:, :].astype(F32) + other_sum_ref[chip ^ k, rows:, :].astype(F32)
+        gain = jnp.sum(tails, axis=0, keepdims=True)
+        out_ref = keep_ref if i < half else send_ref
+        out_ref[i % half, :width, :] = term.astype(BF16)
+        out_ref[i % half, width:, :] = two_parts(gain, ids[0], 2 * n)
+
+
+def pair_sum_kernel(ids, kept_ref, taken_ref, keep_ref, send_ref):
+    half = keep_ref.shape[0]
+    keep_ref[...] = kept_ref[:half].astype(F32) + taken_ref[:half].astype(F32)
+    send_ref[...] = (kept_ref[half:].astype(F32) + taken_ref[half:].astype(F32)).astype(BF16)
+
+
+def assemble_kernel(n, ids, pieces_ref, *outs):
     for i in range(n):
-        proj_ref[i, :width, :] = term[:, i * columns : (i + 1) * columns]
-        proj_ref[i, width:, :] = tail[:, i * columns : (i + 1) * columns]
-
-
-def assemble_kernel(n, ids, *refs):
-    pieces, outs = refs[:n], refs[n:]
-    me = ids[0]
-    width = pieces[0].shape[2]
-    for i in range(n):
-        columns = pl.ds(offset(me ^ i, width), width)
         for part in range(3):
-            outs[part][:, columns] = pieces[i][part].astype(F32)
+            outs[part][:, i * HEAD_DIM : (i + 1) * HEAD_DIM] = pieces_ref[i, part].astype(F32)
 
 
 def swap(x, axis, count, i):
@@ -224,7 +261,10 @@
 
 
 def swap_all(parts, axis, count):
-    return [parts[0]] + [swap(parts[i], axis, count, i) for i in range(1, count)]
+    moved = {0: parts[0]}
+    for i in sorted(range(1, count), key=lambda i: (-(i.bit_length()), i)):
+        moved[i] = swap(parts[i], axis, count, i)
+    return [moved[i] for i in range(count)]
 
 
 def heads_body(n, t, queries, key_rows, value_rows, segment_ids, codebook_ids, code_table, input_proj, norm_gain, upstream):
@@ -239,60 +279,62 @@
     seg = segment_ids.reshape(1, frames)
     piece = (3, rows, HEAD_DIM)
     tall = (frames, HEAD_DIM)
-    w_spec = {0: pl.BlockSpec((width, depth), lambda step, ids: (ids[1], 0))}
-
-    raw = pl.BlockSpec(memory_space=pl.ANY)
-    packed = call(
-        functools.partial(pack_kernel, n, HEAD_DIM),
+
+    (packed,) = call(
+        functools.partial(pack_kernel, n),
         "pack",
-        ids,
+        jnp.zeros((2,), jnp.int32),
         [queries, key_rows, value_rows],
-        [(piece, BF16)] * n,
+        [((n,) + piece, BF16)],
         [pltpu.SemaphoreType.DMA((3 * n,))],
-        in_specs={i: raw for i in range(3)},
-        out_specs={i: raw for i in range(n)},
-    )
-    pieces = swap_all(packed, "ctx", n)
+        in_specs={i: pl.BlockSpec(memory_space=pl.ANY) for i in range(3)},
+        vmem=58,
+    )
+    pieces = lax.all_to_all(packed, "ctx", 0, 0, tiled=True)
 
     codes = [codebook_ids] + [swap(codebook_ids, "tp", t, i) for i in range(1, t)]
     found = call(
         functools.partial(lookup_kernel, t),
         "lookup",
         ids,
-        [code_table] + codes,
-        [((books, local, depth), BF16)] * t,
-        in_specs={0: pl.BlockSpec((1, shard_rows, depth), lambda step, ids: (step, 0, 0))},
-        out_specs={i: pl.BlockSpec((1, local, depth), lambda step, ids: (step, 0, 0)) for i in range(t)},
+        [code_table, input_proj] + codes,
+        [((books, local, depth), BF16)] * t + [((width, depth), BF16)],
+        in_specs={
+            0: pl.BlockSpec((1, shard_rows, depth), lambda step, ids: (step, 0, 0)),
+            1: pl.BlockSpec((width // books, depth), lambda step, ids: (ids[1] * books + step, 0)),
+        },
+        out_specs={i: pl.BlockSpec((1, local, depth), lambda step, ids: (step, 0, 0)) for i in range(t)}
+        | {t: pl.BlockSpec((width // books, depth), lambda step, ids: (step, 0))},
         grid=(books,),
+        vmem=58,
         flops=2 * books * t * local * shard_rows * depth,
     )
-    embedded = sum(x.astype(F32) for x in swap_all(found, "tp", t)).astype(BF16)
+    w_part = found[t]
+    embedded = sum(x.astype(F32) for x in swap_all(found[:t], "tp", t)).astype(BF16)
     cotangent = upstream.transpose(1, 0, 2)
 
     pair_flops = 4 * frames * (window + 1) * rows * HEAD_DIM
-    out_full, norm, query, key, value = call(
+    out_full, norm = call(
         functools.partial(forward_kernel, n, rows, window, factor),
         "attend",
         ids,
-        [seg] + pieces,
-        [(tall, BF16), ((1, frames), F32)] + [(tall, BF16)] * 3,
+        [seg, pieces],
+        [(tall, BF16), ((1, frames), F32)],
         flops=pair_flops,
+        vmem=24,
     )
     out_heads = lax.all_to_all(out_full.reshape(n, rows, HEAD_DIM), "ctx", 0, 0, tiled=True)
     projected = call(
         functools.partial(project_kernel, n, t),
         "project",
         ids,
-        [input_proj, out_heads],
+        [w_part, out_heads],
         [((rows, width), BF16)] + [((local, depth), BF16)] * t,
         [pltpu.VMEM((rows, depth), BF16)],
-        in_specs=w_spec,
         flops=2 * rows * width * depth,
-        extra=2 * width * depth,
-        skip=1,
     )
     attn_out = projected[0]
-    extra_rows = 16
+    extra_rows = 8
     depth_rows, grad_sum = call(
         functools.partial(depth_kernel, t, books),
         "depth",
@@ -301,36 +343,71 @@
         [((books, local, depth), BF16), ((local + extra_rows, depth), BF16)],
     )
     sums = [grad_sum] + [swap(grad_sum, "tp", t, i) for i in range(1, t)]
-    grad_heads, proj_term = call(
+    chunk = (n // 2, rows + 2 * GAIN_SLOTS, depth // n)
+    grad_heads, sums_kept, sums_sent = call(
         functools.partial(grad_attn_kernel, n, t),
         "grad_attn",
         ids,
-        [input_proj, attn_out] + sums,
-        [((n, rows, HEAD_DIM), BF16), ((n, width + 2 * n, depth // n), BF16)],
+        [w_part] + sums,
+        [((n, rows, HEAD_DIM), BF16), (chunk, BF16), (chunk, BF16)],
         [pltpu.VMEM((rows, depth), BF16)],
-        in_specs=w_spec,
-        flops=4 * rows * width * depth,
-        extra=2 * width * depth,
-        skip=1,
-    )
-    proj_sum = lax.psum_scatter(
-        proj_term.reshape(n * (width + 2 * n), depth // n), "ctx", scatter_dimension=0, tiled=True
+        flops=2 * rows * width * depth,
     )
     grad_full = lax.all_to_all(grad_heads, "ctx", 0, 0, tiled=True).reshape(tall)
-    grads = call(
-        functools.partial(backward_kernel, n, rows, window, factor, scale),
+    late_norm, _ = lax.optimization_barrier((norm, grad_heads))
+    pair_rows = rows * sum(min(block, window) + 1 for block in range(n))
+    (probs,) = call(
+        functools.partial(probs_kernel, n, rows, window, factor),
+        "probs",
+        ids,
+        [seg, late_norm, pieces],
+        [((pair_rows, rows), BF16)],
+        flops=pair_flops // 2,
+        vmem=12,
+    )
+    attn_out, probs = lax.optimization_barrier((attn_out, probs))
+    slab = (n // 4, width + 2 * n, depth // n)
+    kept, sent = call(
+        functools.partial(grad_proj_kernel, n),
+        "grad_proj",
+        ids,
+        [attn_out, swap(attn_out, "ctx", n, 1), sums_kept, swap(sums_sent, "ctx", n, 1)],
+        [(slab, BF16)] * 2,
+        flops=2 * rows * width * depth,
+    )
+    sent, grad_full = lax.optimization_barrier((sent, grad_full))
+    taken = swap(sent, "ctx", n, 2)
+    (grads,) = call(
+        functools.partial(backward_kernel, n, rows, window, scale),
         "attend_grad",
         ids,
-        [seg, norm, out_full, query, key, value, grad_full],
-        [(piece, BF16)] * n,
-        [pltpu.VMEM(tall, BF16)] + [pltpu.VMEM(tall, F32)] * 2,
-        flops=5 * pair_flops // 2,
-    )
+        [probs, out_full, pieces, grad_full],
+        [((n,) + piece, BF16)],
+        [pltpu.VMEM(tall, F32)] * 2,
+        costly=False,
+        vmem=20,
+    )
+    step = 4
+    while step < n:
+        half = kept.shape[0] // 2
+        kept, sent = call(
+            pair_sum_kernel,
+            "pair_sum",
+            ids,
+            [kept, taken],
+            [((half,) + kept.shape[1:], F32), ((half,) + kept.shape[1:], BF16)],
+            flops=1 << 36,
+        )
+        taken = swap(sent, "ctx", n, step)
+        step *= 2
+    back = lax.all_to_all(grads, "ctx", 0, 0, tiled=True)
     grad_query, grad_key, grad_value = call(
-        functools.partial(assemble_kernel, n), "assemble", ids, swap_all(grads, "ctx", n), [((rows, width), F32)] * 3
-    )
-    grad_proj = proj_sum[:width].astype(F32)
-    gain = jnp.sum(proj_sum[width:].astype(F32), axis=0)
+        functools.partial(assemble_kernel, n), "assemble", ids, [back], [((rows, width), F32)] * 3
+    )
+    taken, grad_query = lax.optimization_barrier((taken, grad_query))
+    proj_sum = kept[0].astype(F32) + taken[0].astype(F32)
+    grad_proj = proj_sum[:width]
+    gain = jnp.sum(proj_sum[width:], axis=0)
     part = depth // (n * t)
     grad_gain = lax.dynamic_slice_in_dim(gain, lax.axis_index("tp") * part, part, 0)
     return (depth_rows.transpose(1, 0, 2), grad_query, grad_key, grad_value, grad_proj, grad_gain)
@@ -338,7 +415,7 @@
 
 def body(n, t, queries, *rest):
     heads = queries.shape[1] // HEAD_DIM
-    if heads == n and n & (n - 1) == 0 and t & (t - 1) == 0 and n > 1:
+    if heads == n and n & (n - 1) == 0 and t & (t - 1) == 0 and n > 3:
         return heads_body(n, t, queries, *rest)
     return general_body(queries, *rest)
 

time: 200 us -> 186 us (0.930)
  the two profiles are of different devices: /device:TPU:9 before, /device:TPU:0 now
where the time goes in v3:
time: 186 us; the launch traced here: 185 us
  waiting for transfers between devices  87.3 us (47%)
  Pallas kernels  42.6 us (23%)
  starting transfers between devices  34.5 us (19%)
  local copies, waits for them, and re-layouts  15.2 us (8%)
  other arithmetic  4.45 us (2%)
    pallas_call x11, Pallas kernels, call(): pl.pallas_call(kernel, name=name, out_shape=[jax.ShapeDtypeStruct(shape,...  42.6 us
    all_to_all x1, waiting for transfers between devices, heads_body(): back = lax.all_to_all(grads, 'ctx', 0, 0, tiled=True)  36.7 us
    ppermute x16, starting transfers between devices, swap(): return lax.ppermute(x, axis, [(b, b ^ i) for b in range(count)])  17.4 us
    ppermute x16, waiting for transfers between devices, swap(): return lax.ppermute(x, axis, [(b, b ^ i) for b in range(count)])  16.2 us
    all_to_all x1, waiting for transfers between devices, heads_body(): pieces = lax.all_to_all(packed, 'ctx', 0, 0, tiled=True)  15 us
    all_to_all x1, waiting for transfers between devices, heads_body(): lax.all_to_all(out_full.reshape(n, rows, HEAD_DIM), 'ctx', 0, 0, tiled=True)  13.5 us
    unnamed x41, local copies, waits for them, and re-layouts  13.3 us
    all_to_all x1, starting transfers between devices, heads_body(): pieces = lax.all_to_all(packed, 'ctx', 0, 0, tiled=True)  6.34 us
  transfers between devices with their start and end apart: 20, of which 11 were waited for; matrix products, arithmetic and copies ran while one was open for 4% of the time, Pallas kernels for 19%

profile of v3, /device:TPU:0, one launch (start us, length us, event | category | flops | bytes accessed | tf_op | source)
XLA Modules:
  0.0 184.8 jit_solution(11012530439567043369)
XLA Ops:
  1.1 3.5 %pack.1 = bf16[8,3,256,128]{3,2,1,0:T(8,128)(2,1)} custom-call(s32[2]{0:T(128)} %broadcast_1_ids.2.ids, bf16[256,1024]{1,0:T(8,128)(2,1)} %q_ref.1, bf16[256,1024]{1,0:T(8,128)(2,1)} %k_ref.1, bf16[256,1024]{1,0:T(8,128)(2,1)} %v_ref.1), custom_call_target="tpu_custom_call" | custom-call | bytes 3145728 | tf_op jit(solution)/shard_map/pack/pallas_call | solution.py:36
  4.6 6.3 %all-to-all-start = ((bf16[8,3,256,128]{3,2,1,0:T(8,128)(2,1)}), bf16[8,3,256,128]{3,2,1,0:T(8,128)(2,1)S(1)}, u32[]{:S(2)}, u32[]{:S(2)}) async-start(bf16[8,3,256,128]{3,2,1,0:T(8,128)(2,1)} %pack.1), calls=%async_computation | async-start | bytes 3145728 | tf_op jit(solution)/shard_map/all_to_all | solution.py:293
  11.1 1.6 collective-permute-start
  16.5 2.4 %collective-permute-done.2.refs_3_ = s32[64,8]{1,0:T(8,128)S(1)} collective-permute-done((s32[64,8]{1,0:T(8,128)S(1)}, s32[64,8]{1,0:T(8,128)S(1)}, u32[]{:S(2)}, u32[]{:S(2)}) %collective-permute-start.2) | collective-permute-done | bytes 2080 | tf_op jit(solution)/shard_map/ppermute | solution.py:260
  19.6 10.7 %lookup.1 = (bf16[8,64,1024]{2,1,0:T(8,128)(2,1)}, bf16[8,64,1024]{2,1,0:T(8,128)(2,1)}, bf16[8,64,1024]{2,1,0:T(8,128)(2,1)}, bf16[8,64,1024]{2,1,0:T(8,128)(2,1)}, bf16[1024,1024]{1,0:T(8,128)(2,1)}) custom-call(s32[2]{0:T(128)} %pad_add_fusion.ids, bf16[8,512,1024]{2,1,0:T(8,128)(2,1)} %table_ref.1, bf16[4096,1024]{1,0:T(8,128)(2,1)} %w_ref.1, ...), custom_call_target="tpu_custom_call" | custom-call | flops 2147483648 | bytes 23076864 | tf_op jit(solution)/shard_map/lookup/pallas_call | solution.py:36
  33.8 15.0 %all-to-all-done.pieces_ref = bf16[8,3,256,128]{3,2,1,0:T(8,128)(2,1)S(1)} async-done(((bf16[8,3,256,128]{3,2,1,0:T(8,128)(2,1)}), bf16[8,3,256,128]{3,2,1,0:T(8,128)(2,1)S(1)}, u32[]{:S(2)}, u32[]{:S(2)}) %all-to-all-start) | async-done | bytes 1572896 | tf_op jit(solution)/shard_map/all_to_all | solution.py:293
  48.8 6.4 %attend.1 = (bf16[2048,128]{1,0:T(8,128)(2,1)}, f32[1,2048]{1,0:T(1,128)S(1)}) custom-call(s32[2]{0:T(128)S(1)} %copy-done.6, s32[1,2048]{1,0:T(1,128)S(1)} %bitcast.15, bf16[8,3,256,128]{3,2,1,0:T(8,128)(2,1)S(1)} %all-to-all-done.pieces_ref), custom_call_target="tpu_custom_call" | custom-call | flops 1342177280 | bytes 2109440 | tf_op jit(solution)/shard_map/attend/pallas_call | solution.py:36
  55.2 3.5 %all-to-all-start.1 = ((bf16[8,256,128]{2,1,0:T(8,128)(2,1)}), bf16[8,256,128]{2,1,0:T(8,128)(2,1)S(1)}, u32[]{:S(2)}, u32[]{:S(2)}) async-start(bf16[8,256,128]{2,1,0:T(8,128)(2,1)} %bitcast.5), calls=%async_computation.1 | async-start | bytes 1048576 | tf_op jit(solution)/shard_map/all_to_all | solution.py:326
  58.7 1.8 copy.22
  60.6 13.5 %all-to-all-done.1.heads_ref = bf16[8,256,128]{2,1,0:T(8,128)(2,1)S(1)} async-done(((bf16[8,256,128]{2,1,0:T(8,128)(2,1)}), bf16[8,256,128]{2,1,0:T(8,128)(2,1)S(1)}, u32[]{:S(2)}, u32[]{:S(2)}) %all-to-all-start.1) | async-done | bytes 524320 | tf_op jit(solution)/shard_map/all_to_all | solution.py:326
  74.0 1.6 copy-done.2
  81.3 2.8 %add_convert_fusion.embed_ref = bf16[8,64,1024]{2,1,0:T(8,128)(2,1)S(1)} fusion(bf16[8,64,1024]{2,1,0:T(8,128)(2,1)} %collective-permute-done.5, bf16[8,64,1024]{2,1,0:T(8,128)(2,1)} %collective-permute-done.4, bf16[8,64,1024]{2,1,0:T(8,128)(2,1)} %collective-permute-done.3, bf16[8,64,1024]{2,1,0:T(8,128)(2,1)S(1)} %copy-done.13), kind=kLoop, calls=%fused_computation | loop fusion | flops 4194304 | bytes 5242880 | tf_op jit(solution)/shard_map/convert_element_type | solution.py:313
  84.1 3.0 %collective-permute-done.7.refs_2_ = bf16[64,1024]{1,0:T(8,128)(2,1)S(1)} collective-permute-done((bf16[64,1024]{1,0:T(8,128)(2,1)S(1)}, bf16[64,1024]{1,0:T(8,128)(2,1)S(1)}, u32[]{:S(2)}, u32[]{:S(2)}) %collective-permute-start.7) | collective-permute-done | bytes 131104 | tf_op jit(solution)/shard_map/ppermute | solution.py:260
  87.0 1.9 %depth.1 = (bf16[8,64,1024]{2,1,0:T(8,128)(2,1)S(1)}, bf16[72,1024]{1,0:T(8,128)(2,1)S(1)}) custom-call(s32[2]{0:T(128)S(1)} %copy-done.6, f32[1,1024]{1,0:T(1,128)S(1)} %bitcast.17, bf16[8,64,1024]{2,1,0:T(8,128)(2,1)S(1)} %add_convert_fusion.embed_ref, bf16[8,64,1024]{2,1,0:T(8,128)(2,1)S(1)} %bitcast.12, bf16[64,1024]{1,0:T(8,128)(2,1)S(1)} %get-tuple-element.43.refs_0_, ...), custom_call_target="tpu_custom_call" | custom-call | bytes 3821568 | tf_op jit(solution)/shard_map/depth/pallas_call | solution.py:36
  91.7 1.6 collective-permute-start.11
  93.4 2.9 %collective-permute-done.9.refs_1_ = bf16[72,1024]{1,0:T(8,128)(2,1)S(1)} collective-permute-done((bf16[72,1024]{1,0:T(8,128)(2,1)S(1)}, bf16[72,1024]{1,0:T(8,128)(2,1)S(1)}, u32[]{:S(2)}, u32[]{:S(2)}) %collective-permute-start.9) | collective-permute-done | bytes 147488 | tf_op jit(solution)/shard_map/ppermute | solution.py:260
  96.3 2.0 %collective-permute-done.10.refs_2_ = bf16[72,1024]{1,0:T(8,128)(2,1)S(1)} collective-permute-done((bf16[72,1024]{1,0:T(8,128)(2,1)S(1)}, bf16[72,1024]{1,0:T(8,128)(2,1)S(1)}, u32[]{:S(2)}, u32[]{:S(2)}) %collective-permute-start.10) | collective-permute-done | bytes 147488 | tf_op jit(solution)/shard_map/ppermute | solution.py:260
  98.3 2.1 %grad_attn.1 = (bf16[8,256,128]{2,1,0:T(8,128)(2,1)}, bf16[4,272,128]{2,1,0:T(8,128)(2,1)S(1)}, bf16[4,272,128]{2,1,0:T(8,128)(2,1)S(1)}) custom-call(s32[2]{0:T(128)S(1)} %copy-done.6, bf16[1024,1024]{1,0:T(8,128)(2,1)S(1)} %copy-done.3, bf16[72,1024]{1,0:T(8,128)(2,1)S(1)} %get-tuple-element.50.refs_0_, ...), custom_call_target="tpu_custom_call" | custom-call | flops 536870912 | bytes 3768320 | tf_op jit(solution)/shard_map/grad_attn/pallas_call | solution.py:36
  100.4 3.7 %all-to-all-start.2 = ((bf16[8,256,128]{2,1,0:T(8,128)(2,1)}), bf16[8,256,128]{2,1,0:T(8,128)(2,1)S(1)}, u32[]{:S(2)}, u32[]{:S(2)}) async-start(bf16[8,256,128]{2,1,0:T(8,128)(2,1)} %get-tuple-element.51), calls=%async_computation.2 | async-start | bytes 1048576 | tf_op jit(solution)/shard_map/all_to_all | solution.py:356
  104.1 2.4 %probs.1.probs_ref = bf16[7680,256]{1,0:T(8,128)(2,1)S(1)} custom-call(s32[2]{0:T(128)S(1)} %copy-done.6, s32[1,2048]{1,0:T(1,128)S(1)} %bitcast.16, f32[1,2048]{1,0:T(1,128)S(1)} %get-tuple-element.52.norm_ref, bf16[8,3,256,128]{3,2,1,0:T(8,128)(2,1)S(1)} %all-to-all-done.pieces_ref), custom_call_target="tpu_custom_call" | custom-call | flops 671088640 | bytes 5521408 | tf_op jit(solution)/shard_map/probs/pallas_call | solution.py:36
  106.5 1.9 %copy-done = bf16[7680,256]{1,0:T(8,128)(2,1)} copy-done((bf16[7680,256]{1,0:T(8,128)(2,1)}, bf16[7680,256]{1,0:T(8,128)(2,1)S(1)}, u32[]{:S(2)}) %copy-start) | copy-done | bytes 3932184
  108.9 1.8 collective-permute-done.13.other_sum_ref
  110.7 1.8 grad_proj.1
  113.4 5.8 %all-to-all-done.2 = bf16[8,256,128]{2,1,0:T(8,128)(2,1)S(1)} async-done(((bf16[8,256,128]{2,1,0:T(8,128)(2,1)}), bf16[8,256,128]{2,1,0:T(8,128)(2,1)S(1)}, u32[]{:S(2)}, u32[]{:S(2)}) %all-to-all-start.2) | async-done | bytes 524320 | tf_op jit(solution)/shard_map/all_to_all | solution.py:356
  119.2 2.1 %copy-done.1 = bf16[7680,256]{1,0:T(8,128)(2,1)S(1)} copy-done((bf16[7680,256]{1,0:T(8,128)(2,1)S(1)}, bf16[7680,256]{1,0:T(8,128)(2,1)}, u32[]{:S(2)}) %copy-start.1) | copy-done | bytes 3932184
  121.3 8.2 %attend_grad.1 = bf16[8,3,256,128]{3,2,1,0:T(8,128)(2,1)} custom-call(s32[2]{0:T(128)S(1)} %copy-done.6, bf16[7680,256]{1,0:T(8,128)(2,1)S(1)} %copy-done.1, bf16[2048,128]{1,0:T(8,128)(2,1)} %get-tuple-element.42.out_ref, bf16[8,3,256,128]{3,2,1,0:T(8,128)(2,1)S(1)} %all-to-all-done.pieces_ref, bf16[2048,128]{1,0:T(8,128)(2,1)S(1)} %bitcast.13), custom_call_target="tpu_custom_call" | custom-call | tf_op jit(solution)/shard_map/attend_grad/pallas_call | solution.py:36
  129.6 3.6 %all-to-all-start.3 = ((bf16[8,3,256,128]{3,2,1,0:T(8,128)(2,1)}), bf16[8,3,256,128]{3,2,1,0:T(8,128)(2,1)S(1)}, u32[]{:S(2)}, u32[]{:S(2)}) async-start(bf16[8,3,256,128]{3,2,1,0:T(8,128)(2,1)} %attend_grad.1), calls=%async_computation.3 | async-start | bytes 3145728 | tf_op jit(solution)/shard_map/all_to_all | solution.py:403
  134.2 1.7 pair_sum.1
  135.9 2.9 %collective-permute-start.15 = (bf16[1,1040,128]{2,1,0:T(8,128)(2,1)S(1)}, bf16[1,1040,128]{2,1,0:T(8,128)(2,1)}, u32[]{:S(2)}, u32[]{:S(2)}) collective-permute-start(bf16[1,1040,128]{2,1,0:T(8,128)(2,1)S(1)} %get-tuple-element.59), channel_id=1, source_target_pairs={{0,16},{4,20},{8,24},{12,28},{16,0},{20,4},{24,8},{28,12},{1,17},{... | collective-permute-start | bytes 798728 | tf_op jit(solution)/shard_map/ppermute | solution.py:260
  140.4 36.7 %all-to-all-done.3.pieces_ref = bf16[8,3,256,128]{3,2,1,0:T(8,128)(2,1)S(1)} async-done(((bf16[8,3,256,128]{3,2,1,0:T(8,128)(2,1)}), bf16[8,3,256,128]{3,2,1,0:T(8,128)(2,1)S(1)}, u32[]{:S(2)}, u32[]{:S(2)}) %all-to-all-start.3) | async-done | bytes 1572896 | tf_op jit(solution)/shard_map/all_to_all | solution.py:403
  177.1 2.5 %assemble.1 = (f32[256,1024]{1,0:T(8,128)}, f32[256,1024]{1,0:T(8,128)}, f32[256,1024]{1,0:T(8,128)}) custom-call(s32[2]{0:T(128)S(1)} %copy-done.6, bf16[8,3,256,128]{3,2,1,0:T(8,128)(2,1)S(1)} %all-to-all-done.3.pieces_ref), custom_call_target="tpu_custom_call" | custom-call | bytes 3145728 | tf_op jit(solution)/shard_map/assemble/pallas_call | solution.py:36
  179.5 2.9 %collective-permute-done.15 = bf16[1,1040,128]{2,1,0:T(8,128)(2,1)} collective-permute-done((bf16[1,1040,128]{2,1,0:T(8,128)(2,1)S(1)}, bf16[1,1040,128]{2,1,0:T(8,128)(2,1)}, u32[]{:S(2)}, u32[]{:S(2)}) %collective-permute-start.15) | collective-permute-done | bytes 266272 | tf_op jit(solution)/shard_map/ppermute | solution.py:260
  (67 shorter events, 23.4 us)
Async XLA Ops:
  4.6 6.4 %copy-start.18 = (s32[64,8]{0,1:T(8,128)S(1)}, s32[64,8]{0,1:T(8,128)}, u32[]{:S(2)}) copy-start(s32[64,8]{0,1:T(8,128)} %param.13) | copy-start | bytes 6148
  4.6 44.2 %all-to-all-start = ((bf16[8,3,256,128]{3,2,1,0:T(8,128)(2,1)}), bf16[8,3,256,128]{3,2,1,0:T(8,128)(2,1)S(1)}, u32[]{:S(2)}, u32[]{:S(2)}) async-start(bf16[8,3,256,128]{3,2,1,0:T(8,128)(2,1)} %pack.1), calls=%async_computation | async-start | bytes 3145728 | tf_op jit(solution)/shard_map/all_to_all | solution.py:293
  11.1 7.9 %copy-start.14 = (s32[64,8]{1,0:T(8,128)}, s32[64,8]{1,0:T(8,128)S(1)}, u32[]{:S(2)}) copy-start(s32[64,8]{1,0:T(8,128)S(1)} %copy.18.refs_0_) | copy-start | bytes 6148
  11.1 4.2 %collective-permute-start = (s32[64,8]{1,0:T(8,128)S(1)}, s32[64,8]{1,0:T(8,128)S(1)}, u32[]{:S(2)}, u32[]{:S(2)}) collective-permute-start(s32[64,8]{1,0:T(8,128)S(1)} %copy.18.refs_0_), channel_id=1, source_target_pairs={{0,1},{1,0},{2,3},{3,2},{4,5},{5,4},{6,7},{7,6},{8,9},{9,8},{10,11... | collective-permute-start | bytes 6152 | tf_op jit(solution)/shard_map/ppermute | solution.py:260
  12.6 3.9 %collective-permute-start.1 = (s32[64,8]{1,0:T(8,128)S(1)}, s32[64,8]{1,0:T(8,128)S(1)}, u32[]{:S(2)}, u32[]{:S(2)}) collective-permute-start(s32[64,8]{1,0:T(8,128)S(1)} %copy.18.refs_0_), channel_id=1, source_target_pairs={{0,2},{1,3},{2,0},{3,1},{4,6},{5,7},{6,4},{7,5},{8,10},{9,11},{10,... | collective-permute-start | bytes 6152 | tf_op jit(solution)/shard_map/ppermute | solution.py:260
  14.2 4.8 %collective-permute-start.2 = (s32[64,8]{1,0:T(8,128)S(1)}, s32[64,8]{1,0:T(8,128)S(1)}, u32[]{:S(2)}, u32[]{:S(2)}) collective-permute-start(s32[64,8]{1,0:T(8,128)S(1)} %copy.18.refs_0_), channel_id=1, source_target_pairs={{0,3},{1,2},{2,1},{3,0},{4,7},{5,6},{6,5},{7,4},{8,11},{9,10},{10,... | collective-permute-start | bytes 6152 | tf_op jit(solution)/shard_map/ppermute | solution.py:260
  15.3 33.5 %copy-start.6 = (s32[2]{0:T(128)S(1)}, s32[2]{0:T(128)}, u32[]{:S(2)}) copy-start(s32[2]{0:T(128)} %pad_add_fusion.ids) | copy-start | bytes 28
  15.3 33.5 %copy-start.7 = (s32[2048]{0:T(1024)S(1)}, s32[2048]{0:T(1024)}, u32[]{:S(2)}) copy-start(s32[2048]{0:T(1024)} %param.12) | copy-start | bytes 24580
  15.3 3.7 %copy-start.15 = (s32[64,8]{1,0:T(8,128)}, s32[64,8]{1,0:T(8,128)S(1)}, u32[]{:S(2)}) copy-start(s32[64,8]{1,0:T(8,128)S(1)} %collective-permute-done.refs_1_) | copy-start | bytes 6148
  16.5 2.4 %copy-start.16 = (s32[64,8]{1,0:T(8,128)}, s32[64,8]{1,0:T(8,128)S(1)}, u32[]{:S(2)}) copy-start(s32[64,8]{1,0:T(8,128)S(1)} %collective-permute-done.1.refs_2_) | copy-start | bytes 6148
  30.3 50.5 %collective-permute-start.5 = (bf16[8,64,1024]{2,1,0:T(8,128)(2,1)}, bf16[8,64,1024]{2,1,0:T(8,128)(2,1)}, u32[]{:S(2)}, u32[]{:S(2)}) collective-permute-start(bf16[8,64,1024]{2,1,0:T(8,128)(2,1)} %get-tuple-element.40), channel_id=1, source_target_pairs={{0,3},{1,2},{2,1},{3,0},{4,7},{5,6},{6,5},{7,4},{8,11},{9,10},{10,... | collective-permute-start | bytes 3145736 | tf_op jit(solution)/shard_map/ppermute | solution.py:260
  30.8 50.5 %collective-permute-start.4 = (bf16[8,64,1024]{2,1,0:T(8,128)(2,1)}, bf16[8,64,1024]{2,1,0:T(8,128)(2,1)}, u32[]{:S(2)}, u32[]{:S(2)}) collective-permute-start(bf16[8,64,1024]{2,1,0:T(8,128)(2,1)} %get-tuple-element.39), channel_id=1, source_target_pairs={{0,2},{1,3},{2,0},{3,1},{4,6},{5,7},{6,4},{7,5},{8,10},{9,11},{10,... | collective-permute-start | bytes 3145736 | tf_op jit(solution)/shard_map/ppermute | solution.py:260
  32.3 48.9 %collective-permute-start.3 = (bf16[8,64,1024]{2,1,0:T(8,128)(2,1)}, bf16[8,64,1024]{2,1,0:T(8,128)(2,1)}, u32[]{:S(2)}, u32[]{:S(2)}) collective-permute-start(bf16[8,64,1024]{2,1,0:T(8,128)(2,1)} %get-tuple-element.38), channel_id=1, source_target_pairs={{0,1},{1,0},{2,3},{3,2},{4,5},{5,4},{6,7},{7,6},{8,9},{9,8},{10,11... | collective-permute-start | bytes 3145736 | tf_op jit(solution)/shard_map/ppermute | solution.py:260
  55.2 18.8 %all-to-all-start.1 = ((bf16[8,256,128]{2,1,0:T(8,128)(2,1)}), bf16[8,256,128]{2,1,0:T(8,128)(2,1)S(1)}, u32[]{:S(2)}, u32[]{:S(2)}) async-start(bf16[8,256,128]{2,1,0:T(8,128)(2,1)} %bitcast.5), calls=%async_computation.1 | async-start | bytes 1048576 | tf_op jit(solution)/shard_map/all_to_all | solution.py:326
  75.6 5.6 %copy-start.13 = (bf16[8,64,1024]{2,1,0:T(8,128)(2,1)S(1)}, bf16[8,64,1024]{2,1,0:T(8,128)(2,1)}, u32[]{:S(2)}) copy-start(bf16[8,64,1024]{2,1,0:T(8,128)(2,1)} %get-tuple-element.37) | copy-start | bytes 3145732
  77.8 6.3 %collective-permute-start.6 = (bf16[64,1024]{1,0:T(8,128)(2,1)S(1)}, bf16[64,1024]{1,0:T(8,128)(2,1)S(1)}, u32[]{:S(2)}, u32[]{:S(2)}) collective-permute-start(bf16[64,1024]{1,0:T(8,128)(2,1)S(1)} %get-tuple-element.44), channel_id=1, source_target_pairs={{0,1},{1,0},{2,3},{3,2},{4,5},{5,4},{6,7},{7,6},{8,9},{9,8},{10,11... | collective-permute-start | bytes 393224 | tf_op jit(solution)/shard_map/ppermute | solution.py:260
  79.2 7.8 %collective-permute-start.7 = (bf16[64,1024]{1,0:T(8,128)(2,1)S(1)}, bf16[64,1024]{1,0:T(8,128)(2,1)S(1)}, u32[]{:S(2)}, u32[]{:S(2)}) collective-permute-start(bf16[64,1024]{1,0:T(8,128)(2,1)S(1)} %get-tuple-element.45), channel_id=1, source_target_pairs={{0,2},{1,3},{2,0},{3,1},{4,6},{5,7},{6,4},{7,5},{8,10},{9,11},{10,... | collective-permute-start | bytes 393224 | tf_op jit(solution)/shard_map/ppermute | solution.py:260
  80.8 6.3 %collective-permute-start.8 = (bf16[64,1024]{1,0:T(8,128)(2,1)S(1)}, bf16[64,1024]{1,0:T(8,128)(2,1)S(1)}, u32[]{:S(2)}, u32[]{:S(2)}) collective-permute-start(bf16[64,1024]{1,0:T(8,128)(2,1)S(1)} %get-tuple-element.46), channel_id=1, source_target_pairs={{0,3},{1,2},{2,1},{3,0},{4,7},{5,6},{6,5},{7,4},{8,11},{9,10},{10,... | collective-permute-start | bytes 393224 | tf_op jit(solution)/shard_map/ppermute | solution.py:260
  81.3 5.8 %copy-start.8 = (f32[1024]{0:T(1024)S(1)}, f32[1024]{0:T(1024)}, u32[]{:S(2)}) copy-start(f32[1024]{0:T(1024)} %param.16) | copy-start | bytes 12292
  84.0 14.3 %copy-start.3 = (bf16[1024,1024]{1,0:T(8,128)(2,1)S(1)}, bf16[1024,1024]{1,0:T(8,128)(2,1)}, u32[]{:S(2)}) copy-start(bf16[1024,1024]{1,0:T(8,128)(2,1)} %get-tuple-element.41.w_ref) | copy-start | bytes 6291460
  89.9 6.4 %collective-permute-start.9 = (bf16[72,1024]{1,0:T(8,128)(2,1)S(1)}, bf16[72,1024]{1,0:T(8,128)(2,1)S(1)}, u32[]{:S(2)}, u32[]{:S(2)}) collective-permute-start(bf16[72,1024]{1,0:T(8,128)(2,1)S(1)} %get-tuple-element.50.refs_0_), channel_id=1, source_target_pairs={{0,1},{1,0},{2,3},{3,2},{4,5},{5,4},{6,7},{7,6},{8,9},{9,8},{10,11... | collective-permute-start | bytes 442376 | tf_op jit(solution)/shard_map/ppermute | solution.py:260
  90.9 7.4 %collective-permute-start.10 = (bf16[72,1024]{1,0:T(8,128)(2,1)S(1)}, bf16[72,1024]{1,0:T(8,128)(2,1)S(1)}, u32[]{:S(2)}, u32[]{:S(2)}) collective-permute-start(bf16[72,1024]{1,0:T(8,128)(2,1)S(1)} %get-tuple-element.50.refs_0_), channel_id=1, source_target_pairs={{0,2},{1,3},{2,0},{3,1},{4,6},{5,7},{6,4},{7,5},{8,10},{9,11},{10,... | collective-permute-start | bytes 442376 | tf_op jit(solution)/shard_map/ppermute | solution.py:260
  91.7 6.6 %collective-permute-start.11 = (bf16[72,1024]{1,0:T(8,128)(2,1)S(1)}, bf16[72,1024]{1,0:T(8,128)(2,1)S(1)}, u32[]{:S(2)}, u32[]{:S(2)}) collective-permute-start(bf16[72,1024]{1,0:T(8,128)(2,1)S(1)} %get-tuple-element.50.refs_0_), channel_id=1, source_target_pairs={{0,3},{1,2},{2,1},{3,0},{4,7},{5,6},{6,5},{7,4},{8,11},{9,10},{10,... | collective-permute-start | bytes 442376 | tf_op jit(solution)/shard_map/ppermute | solution.py:260
  100.4 18.8 %all-to-all-start.2 = ((bf16[8,256,128]{2,1,0:T(8,128)(2,1)}), bf16[8,256,128]{2,1,0:T(8,128)(2,1)S(1)}, u32[]{:S(2)}, u32[]{:S(2)}) async-start(bf16[8,256,128]{2,1,0:T(8,128)(2,1)} %get-tuple-element.51), calls=%async_computation.2 | async-start | bytes 1048576 | tf_op jit(solution)/shard_map/all_to_all | solution.py:356
  104.1 4.3 %copy-start.10 = (bf16[256,1024]{1,0:T(8,128)(2,1)S(1)}, bf16[256,1024]{1,0:T(8,128)(2,1)}, u32[]{:S(2)}) copy-start(bf16[256,1024]{1,0:T(8,128)(2,1)} %copy-done.9) | copy-start | bytes 1572868
  108.4 2.3 %collective-permute-start.12 = (bf16[256,1024]{1,0:T(8,128)(2,1)S(1)}, bf16[256,1024]{1,0:T(8,128)(2,1)S(1)}, u32[]{:S(2)}, u32[]{:S(2)}) collective-permute-start(bf16[256,1024]{1,0:T(8,128)(2,1)S(1)} %copy-done.10), channel_id=1, source_target_pairs={{0,4},{4,0},{8,12},{12,8},{16,20},{20,16},{24,28},{28,24},{1,5},{5... | collective-permute-start | bytes 1572872 | tf_op jit(solution)/shard_map/ppermute | solution.py:260
  108.6 2.1 %collective-permute-start.13 = (bf16[4,272,128]{2,1,0:T(8,128)(2,1)S(1)}, bf16[4,272,128]{2,1,0:T(8,128)(2,1)S(1)}, u32[]{:S(2)}, u32[]{:S(2)}) collective-permute-start(bf16[4,272,128]{2,1,0:T(8,128)(2,1)S(1)} %get-tuple-element.55), channel_id=1, source_target_pairs={{0,4},{4,0},{8,12},{12,8},{16,20},{20,16},{24,28},{28,24},{1,5},{5... | collective-permute-start | bytes 835592 | tf_op jit(solution)/shard_map/ppermute | solution.py:260
  119.2 13.9 %collective-permute-start.14 = (bf16[2,1040,128]{2,1,0:T(8,128)(2,1)S(1)}, bf16[2,1040,128]{2,1,0:T(8,128)(2,1)}, u32[]{:S(2)}, u32[]{:S(2)}) collective-permute-start(bf16[2,1040,128]{2,1,0:T(8,128)(2,1)S(1)} %get-tuple-element.58), channel_id=1, source_target_pairs={{0,8},{4,12},{8,0},{12,4},{16,24},{20,28},{24,16},{28,20},{1,9},{5... | collective-permute-start | bytes 1597448 | tf_op jit(solution)/shard_map/ppermute | solution.py:260
  119.2 2.1 %copy-start.1 = (bf16[7680,256]{1,0:T(8,128)(2,1)S(1)}, bf16[7680,256]{1,0:T(8,128)(2,1)}, u32[]{:S(2)}) copy-start(bf16[7680,256]{1,0:T(8,128)(2,1)} %copy-done) | copy-start | bytes 11796484
  129.6 47.5 %all-to-all-start.3 = ((bf16[8,3,256,128]{3,2,1,0:T(8,128)(2,1)}), bf16[8,3,256,128]{3,2,1,0:T(8,128)(2,1)S(1)}, u32[]{:S(2)}, u32[]{:S(2)}) async-start(bf16[8,3,256,128]{3,2,1,0:T(8,128)(2,1)} %attend_grad.1), calls=%async_computation.3 | async-start | bytes 3145728 | tf_op jit(solution)/shard_map/all_to_all | solution.py:403
  134.2 4.6 %copy-start.5 = (bf16[8,64,1024]{2,1,0:T(8,128)(2,1)S(1)}, bf16[8,64,1024]{2,1,0:T(8,128)(2,1)}, u32[]{:S(2)}) copy-start(bf16[8,64,1024]{2,1,0:T(8,128)(2,1)} %copy-done.4) | copy-start | bytes 3145732
  135.9 46.5 %collective-permute-start.15 = (bf16[1,1040,128]{2,1,0:T(8,128)(2,1)S(1)}, bf16[1,1040,128]{2,1,0:T(8,128)(2,1)}, u32[]{:S(2)}, u32[]{:S(2)}) collective-permute-start(bf16[1,1040,128]{2,1,0:T(8,128)(2,1)S(1)} %get-tuple-element.59), channel_id=1, source_target_pairs={{0,16},{4,20},{8,24},{12,28},{16,0},{20,4},{24,8},{28,12},{1,17},{... | collective-permute-start | bytes 798728 | tf_op jit(solution)/shard_map/ppermute | solution.py:260
  (7 other events, 7.7 us)
